TPU v7x, 32 devices: a whole 2x2x4 slice. The times are simulated.
32 devices in a mesh: ctx: 8 (over z, x), tp: 4 (over y, core).
Axes of the slice: x: 2, y: 2, z: 4, core: 2. Of those that a mesh axis runs over, the one named last changes fastest.
Arguments:
- residual: bfloat16 [1024, 4096], P('ctx', 'tp')
- mixer_input: bfloat16 [1024, 4096], P('ctx', 'tp')
- gate_input: bfloat16 [1024, 4096], P('ctx', 'tp'), may hold values from -6 to 6
- state_proj: bfloat16 [1024, 32], P('ctx'), may hold values from -6 to 6
- step_raw: float32 [1024, 64], P('ctx', 'tp'), may hold values from -5 to 5
- conv_weight: float32 [4, 4096], P(None, 'tp'), may hold values from -3 to 3
- conv_state_weight: float32 [4, 32], replicated, may hold values from -3 to 3
- step_bias: float32 [64], P('tp'), may hold values from -3.5 to 0.5
- decay_log: float32 [64], P('tp')
- skip_gain: float32 [64], P('tp'), may hold values from 0.5 to 1.5
- mixer_gain: float32 [4096], P('tp'), may hold values from 0.5 to 1.5
- out_weight: bfloat16 [4096, 4096], P('tp', 'ctx'), may hold values from -0.09375 to 0.09375
- feed_gain: float32 [4096], P('tp'), may hold values from 0.5 to 1.5
- expert_gate: bfloat16 [8, 4096, 7168], P('ctx', 'tp'), may hold values from -0.09375 to 0.09375
- expert_up: bfloat16 [8, 4096, 7168], P('ctx', 'tp'), may hold values from -0.09375 to 0.09375
- expert_down: bfloat16 [8, 7168, 4096], P('ctx', None, 'tp'), may hold values from -0.0625 to 0.0625
- expert_ids: int32 [1024, 2], P('ctx'), may hold values from 0 to 7, all different within a row; in each aligned block of 128 rows (0 to 127, 128 to 255, ...) at most 36 rows name the same one
- expert_weights: float32 [1024, 2], P('ctx'), may hold values from 0.1 to 0.9
Outputs:
- block_out: bfloat16 [1024, 4096], P('ctx', 'tp')
Inputs may be any that keep to these rules, and one draw needn't show every extreme that they name: `expert_ids`: in each aligned block of 128 rows no expert is named more than 36 times, and some block reaches 36; the two experts of a row differ.
All inputs are finite; a program needn't handle non-finite values.
Results may differ from a plain program's by a relative error of at most 0.014.
Values may be sent and summed in bfloat16 or wider, within the bound.
A program may use at most 128 MiB of HBM per device.

v0:
```python
import jax
import jax.numpy as jnp
from jax import lax
from jax.sharding import PartitionSpec as P


EXPERTS = 8
CAP = 36


EPSILON = 1e-05


def passed_along(value, axis, steps):
    count = lax.axis_size(axis)
    first, last = (max(0, -steps), min(count, count - steps))
    return lax.ppermute(value, axis, [(source, source + steps) for source in range(first, last)])


def swapped(value, distance):
    return lax.ppermute(value, "tp", [(p, p ^ distance) for p in range(lax.axis_size("tp"))])


def rotated(value, steps):
    count = lax.axis_size("ctx")
    return lax.ppermute(value, "ctx", [(c, (c + steps) % count) for c in range(count)])


def tensor_total(value):
    return (value + swapped(value, 1)) + (swapped(value, 2) + swapped(value, 3))


def entering(decay, fresh, axis):
    peers, position = (lax.axis_size(axis), lax.axis_index(axis))
    packed = jnp.concatenate([fresh, decay[None, :]], axis=0).astype(jnp.bfloat16)
    if peers == EXPERTS:
        total, carry = (jnp.zeros_like(fresh), jnp.ones_like(decay)[None, :])
        for distance in range(1, peers):
            part = passed_along(packed, axis, distance).astype(jnp.float32)
            total = total + carry * part[:-1]
            carry = carry * part[-1:]
        return total
    everything = lax.all_gather(packed, axis).astype(jnp.float32)

    def step(k, before):
        part = everything[k]
        return jnp.where(k < position, part[-1:] * before + part[:-1], before)

    return lax.fori_loop(0, peers, step, jnp.zeros_like(fresh))


def causal_filter(previous, current, kernel):
    joined = jnp.concatenate([previous, current], axis=0)
    length = current.shape[0]
    total = jnp.zeros(current.shape, jnp.float32)
    for offset in range(kernel.shape[0]):
        total = total + kernel[offset][None, :] * joined[offset : offset + length]
    return jax.nn.silu(total)


def local_terms(values, writer, reader, step_size, log_decay):
    length = values.shape[0]
    cumulative = jnp.cumsum(log_decay, axis=0)
    scores = jnp.dot(reader, writer.T, precision=lax.Precision.HIGHEST)
    order = jnp.arange(length)
    causal = (order[:, None] >= order[None, :])[:, :, None]
    spans = cumulative[:, None, :] - cumulative[None, :, :]
    factor = jnp.where(causal, jnp.exp(jnp.where(causal, spans, 0.0)), 0.0)
    factor = factor * step_size[None, :, :] * scores[:, :, None]
    inside = jnp.einsum("tsh,shp->thp", factor, values, precision=lax.Precision.HIGHEST)
    tail = cumulative[length - 1]
    ending = jnp.exp(tail[None, :] - cumulative) * step_size
    weighted = (ending[:, :, None] * values).reshape(length, -1)
    fresh = jnp.dot(writer.T, weighted, precision=lax.Precision.HIGHEST)
    return (inside, cumulative, fresh, tail)


def body(
    residual,
    mixer_input,
    gate_input,
    state_proj,
    step_raw,
    conv_weight,
    conv_state_weight,
    step_bias,
    decay_log,
    skip_gain,
    mixer_gain,
    out_weight,
    feed_gain,
    expert_gate,
    expert_up,
    expert_down,
    expert_ids,
    expert_weights,
):
    tensor_count = lax.axis_size("tp")
    context_count = lax.axis_size("ctx")
    tokens = mixer_input.shape[0]
    channels = mixer_input.shape[1]
    states = state_proj.shape[1] // 2
    heads_local = step_raw.shape[1]
    head_size = channels // heads_local
    taps = conv_weight.shape[0]
    joined = jnp.concatenate([mixer_input, state_proj], axis=1)
    previous = passed_along(joined[tokens - (taps - 1) :], "ctx", 1)
    kernel = jnp.concatenate([conv_weight, conv_state_weight], axis=1)
    filtered = causal_filter(previous.astype(jnp.float32), joined.astype(jnp.float32), kernel)
    values = filtered[:, :channels].reshape(tokens, heads_local, head_size)
    writer = filtered[:, channels : channels + states]
    reader = filtered[:, channels + states :]
    step_size = jax.nn.softplus(step_raw + step_bias[None, :])
    log_decay = -step_size * jnp.exp(decay_log)[None, :]
    inside, cumulative, fresh, tail = local_terms(values, writer, reader, step_size, log_decay)

    incoming = entering(jnp.repeat(jnp.exp(tail), head_size), fresh, "ctx")
    carried = (
        jnp.dot(reader, incoming, precision=lax.Precision.HIGHEST).reshape(values.shape)
        * jnp.exp(cumulative)[:, :, None]
    )
    mixed = inside + carried + skip_gain[None, :, None] * values
    gated = mixed.reshape(tokens, channels) * jax.nn.silu(gate_input.astype(jnp.float32))
    tp_index = lax.axis_index("tp")
    core, chip = (tp_index % 2, tp_index // 2)
    scaled = (gated * mixer_gain[None, :]).astype(jnp.bfloat16)
    direct = context_count == EXPERTS
    ctx_index = lax.axis_index("ctx")
    if direct:
        pairs = []
        for plane in range(4):
            block = rotated(scaled, 2 * plane) if plane else scaled
            other = lax.ppermute(block, "ctx", [(c, c ^ 1) for c in range(context_count)])
            pair = jnp.concatenate([block, other], axis=0)
            pairs.append(jnp.dot(pair, out_weight, preferred_element_type=jnp.float32))
        products = jnp.stack(pairs)

        def projected(quarter):
            place = (ctx_index // 2 - quarter) % 4
            return lax.dynamic_index_in_dim(products, place, 0, keepdims=False)

    else:
        everyone = lax.all_gather(scaled, "ctx", axis=0, tiled=True)
        span = everyone.shape[0] // tensor_count

        def projected(quarter):
            rows = lax.dynamic_slice_in_dim(everyone, quarter * span, span, 0)
            return jnp.dot(rows, out_weight, preferred_element_type=jnp.float32)

    square_sum = tensor_total(jnp.sum(gated * gated, axis=1))
    scale = lax.rsqrt(square_sum / (channels * tensor_count) + EPSILON)
    own, beside = (chip * 2 + core, chip * 2 + 1 - core)
    across, diagonal = ((1 - chip) * 2 + core, (1 - chip) * 2 + 1 - core)
    far = swapped(projected(diagonal).astype(jnp.bfloat16), 1)
    far = swapped((projected(across) + far.astype(jnp.float32)).astype(jnp.bfloat16), 2)
    near = swapped(projected(beside).astype(jnp.bfloat16), 1)
    reduced = projected(own) + near.astype(jnp.float32) + far.astype(jnp.float32)
    blocks = context_count // tensor_count
    reduced = reduced.astype(jnp.bfloat16).reshape(blocks, tokens, -1)
    pieces = []
    for j in range(blocks):
        moves = [
            (c * tensor_count + p, (p * blocks + (c + j) % blocks) * tensor_count + c // blocks)
            for c in range(context_count)
            for p in range(tensor_count)
        ]
        if direct:
            block = reduced[j]
        else:
            block = lax.dynamic_index_in_dim(reduced, (ctx_index + j) % blocks, 0, keepdims=False)
        pieces.append(lax.ppermute(block, ("ctx", "tp"), moves))
    stacked = jnp.stack(pieces)
    order = (ctx_index - jnp.arange(blocks)) % blocks
    if blocks == 2:
        first = ctx_index % 2 == 0
        mixer_out = jnp.concatenate(
            [jnp.where(first, pieces[0], pieces[1]), jnp.where(first, pieces[1], pieces[0])], axis=1
        )
    else:
        mixer_out = jnp.take(stacked, order, axis=0).transpose(1, 0, 2).reshape(tokens, -1)
    mixer_out = mixer_out.astype(jnp.float32) * scale[:, None]
    hidden_state = (residual.astype(jnp.float32) + mixer_out).astype(jnp.bfloat16)
    state_float = lax.optimization_barrier(hidden_state).astype(jnp.float32)
    width_total = hidden_state.shape[1] * tensor_count
    feed_sum = tensor_total(jnp.sum(state_float * state_float, axis=1))
    feed_scale = lax.rsqrt(feed_sum / width_total + EPSILON)
    expert_input = (state_float * feed_scale[:, None] * feed_gain[None, :]).astype(jnp.bfloat16)
    group = context_count // EXPERTS
    width_local = expert_input.shape[1]
    flat_experts = expert_ids.reshape(-1)
    matches = (flat_experts[:, None] == jnp.arange(EXPERTS)[None, :]).astype(jnp.int32)
    slots = jnp.sum((jnp.cumsum(matches, axis=0) - matches) * matches, axis=1)
    places = (flat_experts - ctx_index) % EXPERTS if direct else flat_experts
    targets = (places * CAP + slots).reshape(tokens, -1)
    picker = jnp.any(targets[None, :, :] == jnp.arange(EXPERTS * CAP)[:, None, None], axis=2)
    buffer = jnp.dot(
        picker.astype(jnp.bfloat16), expert_input, preferred_element_type=jnp.float32
    ).astype(jnp.bfloat16)
    outgoing = jnp.broadcast_to(
        buffer.reshape(EXPERTS, 1, CAP, width_local), (EXPERTS, group, CAP, width_local)
    )
    outgoing = outgoing.reshape(EXPERTS * group, CAP, width_local)
    gate_local = expert_gate[0]
    up_local = expert_up[0]
    down_local = expert_down[0]
    sources, items, depth = outgoing.shape
    if direct:
        flattened = jnp.concatenate(
            [outgoing[r] if r == 0 else rotated(outgoing[r], r) for r in range(sources)], axis=0
        )
    else:
        arrived = lax.all_to_all(outgoing, "ctx", split_axis=0, concat_axis=0, tiled=True)
        flattened = arrived.reshape(sources * items, depth)
    hidden = gate_local.shape[1] // tensor_count

    def product(source, weight, quarter):
        columns = lax.dynamic_slice_in_dim(weight, quarter * hidden, hidden, 1)
        return jnp.dot(source, columns, preferred_element_type=jnp.float32)

    fars, nears, rows = ([], [], flattened)
    for weight in (gate_local, up_local):
        far = product(rows, weight, diagonal).astype(jnp.bfloat16)
        far = swapped(far, 1)
        nears.append(swapped(product(rows, weight, beside).astype(jnp.bfloat16), 1))
        far = (product(rows, weight, across) + far.astype(jnp.float32)).astype(jnp.bfloat16)
        far, rows = lax.optimization_barrier((far, rows))
        fars.append(swapped(far, 2))
    gate_share, up_share = (
        product(rows, weight, own).astype(jnp.bfloat16).astype(jnp.float32)
        + near.astype(jnp.float32)
        + far.astype(jnp.float32)
        for weight, near, far in zip((gate_local, up_local), nears, fars)
    )
    share = (jax.nn.silu(gate_share) * up_share).astype(jnp.bfloat16)
    share_across = swapped(share, 2)
    share_beside = swapped(share, 1)

    def lowered(part, quarter):
        rows = lax.dynamic_slice_in_dim(down_local, quarter * hidden, hidden, 0)
        return jnp.dot(part, rows, preferred_element_type=jnp.float32)

    local = lowered(share, own) + lowered(share_beside, beside)
    local, share_across = lax.optimization_barrier((local, share_across))
    share_diagonal = swapped(share_across, 1)
    answer = (
        local
        + lowered(share_across, across)
        + lowered(share_diagonal, diagonal)
    ).astype(jnp.bfloat16)
    answer = answer.reshape(sources, items, depth)
    if direct:
        answers = jnp.stack(
            [answer[r] if r == 0 else rotated(answer[r], -r) for r in range(sources)]
        )
    else:
        answers = lax.all_to_all(answer, "ctx", split_axis=0, concat_axis=0, tiled=True)
    summed = jnp.sum(answers.reshape(EXPERTS, group, CAP, width_local), axis=1, dtype=jnp.float32)
    summed = summed.reshape(EXPERTS * CAP, width_local)
    chosen = jnp.take(summed, targets, axis=0)
    routed = jnp.sum(expert_weights[:, :, None] * chosen, axis=1)
    return (state_float + routed).astype(jnp.bfloat16)


def solution(mesh):
    placed = (
        P("ctx", "tp"),
        P("ctx", "tp"),
        P("ctx", "tp"),
        P("ctx", None),
        P("ctx", "tp"),
        P(None, "tp"),
        P(),
        P("tp"),
        P("tp"),
        P("tp"),
        P("tp"),
        P("tp", "ctx"),
        P("tp"),
        P("ctx", "tp", None),
        P("ctx", "tp", None),
        P("ctx", None, "tp"),
        P("ctx", None),
        P("ctx", None),
    )

    return jax.shard_map(
        body, mesh=mesh, in_specs=placed, out_specs=P("ctx", "tp"), check_vma=False
    )
```

profile of v0, /device:TPU:0, one launch (start us, length us, event | category | flops | bytes accessed | tf_op | source)
XLA Modules:
  0.0 260.8 jit_solution(17155384476702183162)
XLA Ops:
  2.1 4.9 %collective-permute-start = (bf16[3,1056]{0,1:T(8,128)(2,1)S(1)}, bf16[3,1056]{0,1:T(8,128)(2,1)S(1)}, u32[]{:S(2)}, u32[]{:S(2)}) collective-permute-start(bf16[3,1056]{0,1:T(8,128)(2,1)S(1)} %fusion.122), channel_id=1, source_target_pairs={{0,4},{4,8},{8,12},{12,16},{16,20},{20,24},{24,28},{1,5},{5,9},{9,... | collective-permute-start | bytes 19016 | tf_op jit(solution)/shard_map/ppermute | solution.py:17
  9.9 2.8 %collective-permute-done = bf16[3,1056]{0,1:T(8,128)(2,1)S(1)} collective-permute-done((bf16[3,1056]{0,1:T(8,128)(2,1)S(1)}, bf16[3,1056]{0,1:T(8,128)(2,1)S(1)}, u32[]{:S(2)}, u32[]{:S(2)}) %collective-permute-start) | collective-permute-done | bytes 6368 | tf_op jit(solution)/shard_map/ppermute | solution.py:17
  14.8 4.4 %collective-permute-start.1 = (bf16[17,1024]{1,0:T(8,128)(2,1)S(1)}, bf16[17,1024]{1,0:T(8,128)(2,1)S(1)}, u32[]{:S(2)}, u32[]{:S(2)}) collective-permute-start(bf16[17,1024]{1,0:T(8,128)(2,1)S(1)} %pad_maximum_fusion.3), channel_id=1, source_target_pairs={{0,4},{4,8},{8,12},{12,16},{16,20},{20,24},{24,28},{1,5},{5,9},{9,... | collective-permute-start | bytes 104456 | tf_op jit(solution)/shard_map/ppermute | solution.py:17
  19.3 3.5 %collective-permute-start.2 = (bf16[17,1024]{1,0:T(8,128)(2,1)S(1)}, bf16[17,1024]{1,0:T(8,128)(2,1)S(1)}, u32[]{:S(2)}, u32[]{:S(2)}) collective-permute-start(bf16[17,1024]{1,0:T(8,128)(2,1)S(1)} %pad_maximum_fusion.3), channel_id=1, source_target_pairs={{0,8},{4,12},{8,16},{12,20},{16,24},{20,28},{1,9},{5,13},{9,17},{1... | collective-permute-start | bytes 104456 | tf_op jit(solution)/shard_map/ppermute | solution.py:17
  22.8 5.4 %collective-permute-start.3 = (bf16[17,1024]{1,0:T(8,128)(2,1)S(1)}, bf16[17,1024]{1,0:T(8,128)(2,1)S(1)}, u32[]{:S(2)}, u32[]{:S(2)}) collective-permute-start(bf16[17,1024]{1,0:T(8,128)(2,1)S(1)} %pad_maximum_fusion.3), channel_id=1, source_target_pairs={{0,12},{4,16},{8,20},{12,24},{16,28},{1,13},{5,17},{9,21},{13,25},... | collective-permute-start | bytes 104456 | tf_op jit(solution)/shard_map/ppermute | solution.py:17
  33.9 1.6 collective-permute-done.7
  36.5 2.2 fusion.76
  39.4 3.1 %collective-permute-start.11 = (bf16[128,1024]{1,0:T(8,128)(2,1)S(1)}, bf16[128,1024]{1,0:T(8,128)(2,1)S(1)}, u32[]{:S(2)}, u32[]{:S(2)}) collective-permute-start(bf16[128,1024]{1,0:T(8,128)(2,1)S(1)} %get-tuple-element.33), channel_id=1, source_target_pairs={{0,16},{4,20},{8,24},{12,28},{16,0},{20,4},{24,8},{28,12},{1,17},{... | collective-permute-start | bytes 786440 | tf_op jit(solution)/shard_map/ppermute | solution.py:26
  43.2 2.4 collective-permute-start.8
  45.5 4.9 %collective-permute-done.9 = bf16[128,1024]{1,0:T(8,128)(2,1)S(1)} collective-permute-done((bf16[128,1024]{1,0:T(8,128)(2,1)S(1)}, bf16[128,1024]{1,0:T(8,128)(2,1)S(1)}, u32[]{:S(2)}, u32[]{:S(2)}) %collective-permute-start.9) | collective-permute-done | bytes 262176 | tf_op jit(solution)/shard_map/ppermute | solution.py:26
  50.4 1.7 collective-permute-start.10
  52.5 5.8 %collective-permute-done.11 = bf16[128,1024]{1,0:T(8,128)(2,1)S(1)} collective-permute-done((bf16[128,1024]{1,0:T(8,128)(2,1)S(1)}, bf16[128,1024]{1,0:T(8,128)(2,1)S(1)}, u32[]{:S(2)}, u32[]{:S(2)}) %collective-permute-start.11) | collective-permute-done | bytes 262176 | tf_op jit(solution)/shard_map/ppermute | solution.py:26
  58.3 1.8 collective-permute-start.12
  61.3 6.3 %collective-permute-done.12 = bf16[128,1024]{1,0:T(8,128)(2,1)S(1)} collective-permute-done((bf16[128,1024]{1,0:T(8,128)(2,1)S(1)}, bf16[128,1024]{1,0:T(8,128)(2,1)S(1)}, u32[]{:S(2)}, u32[]{:S(2)}) %collective-permute-start.12) | collective-permute-done | bytes 262176 | tf_op jit(solution)/shard_map/ppermute | solution.py:133
  68.0 4.2 %collective-permute-done.14 = bf16[128,1024]{1,0:T(8,128)(2,1)S(1)} collective-permute-done((bf16[128,1024]{1,0:T(8,128)(2,1)S(1)}, bf16[128,1024]{1,0:T(8,128)(2,1)S(1)}, u32[]{:S(2)}, u32[]{:S(2)}) %collective-permute-start.14) | collective-permute-done | bytes 262176 | tf_op jit(solution)/shard_map/ppermute | solution.py:133
  79.1 4.8 %collective-permute-done.17 = bf16[256,512]{1,0:T(8,128)(2,1)S(1)} collective-permute-done((bf16[256,512]{1,0:T(8,128)(2,1)}, bf16[256,512]{1,0:T(8,128)(2,1)S(1)}, u32[]{:S(2)}, u32[]{:S(2)}) %collective-permute-start.17) | collective-permute-done | bytes 262176 | tf_op jit(solution)/shard_map/ppermute | solution.py:21
  84.7 1.8 collective-permute-start.19
  86.5 3.2 %collective-permute-done.19 = bf16[128,512]{1,0:T(8,128)(2,1)S(1)} collective-permute-done((bf16[128,512]{1,0:T(8,128)(2,1)S(1)}, bf16[128,512]{1,0:T(8,128)(2,1)S(1)}, u32[]{:S(2)}, u32[]{:S(2)}) %collective-permute-start.19) | collective-permute-done | bytes 131104 | tf_op jit(solution)/shard_map/ppermute | solution.py:171
  90.0 5.9 %collective-permute-start.23 = (f32[128]{0:T(128)S(1)}, f32[128]{0:T(128)S(1)}, u32[]{:S(2)}, u32[]{:S(2)}) collective-permute-start(f32[128]{0:T(128)S(1)} %fusion.95), channel_id=1, source_target_pairs={{0,1},{1,0},{2,3},{3,2},{4,5},{5,4},{6,7},{7,6},{8,9},{9,8},{10,11... | collective-permute-start | bytes 1544 | tf_op jit(solution)/shard_map/ppermute | solution.py:21
  96.0 9.4 %collective-permute-start.24 = (f32[128]{0:T(128)S(1)}, f32[128]{0:T(128)S(1)}, u32[]{:S(2)}, u32[]{:S(2)}) collective-permute-start(f32[128]{0:T(128)S(1)} %fusion.95), channel_id=1, source_target_pairs={{0,2},{1,3},{2,0},{3,1},{4,6},{5,7},{6,4},{7,5},{8,10},{9,11},{10,... | collective-permute-start | bytes 1544 | tf_op jit(solution)/shard_map/ppermute | solution.py:21
  110.5 4.3 %collective-permute-start.29 = (bf16[36,1024]{1,0:T(8,128)(2,1)S(1)}, bf16[36,1024]{1,0:T(8,128)(2,1)S(1)}, u32[]{:S(2)}, u32[]{:S(2)}) collective-permute-start(bf16[36,1024]{1,0:T(8,128)(2,1)S(1)} %get-tuple-element.44), channel_id=1, source_target_pairs={{0,16},{4,20},{8,24},{12,28},{16,0},{20,4},{24,8},{28,12},{1,17},{... | collective-permute-start | bytes 221192 | tf_op jit(solution)/shard_map/ppermute | solution.py:26
  114.8 2.2 collective-permute-done.26
  117.2 2.3 collective-permute-start.32
  119.5 3.8 %collective-permute-done.28 = bf16[36,1024]{1,0:T(8,128)(2,1)S(1)} collective-permute-done((bf16[36,1024]{1,0:T(8,128)(2,1)S(1)}, bf16[36,1024]{1,0:T(8,128)(2,1)S(1)}, u32[]{:S(2)}, u32[]{:S(2)}) %collective-permute-start.28) | collective-permute-done | bytes 73760 | tf_op jit(solution)/shard_map/ppermute | solution.py:26
  125.7 3.5 %fusion.48 = bf16[288,1792]{1,0:T(8,128)(2,1)S(1)} fusion(bf16[288,1024]{1,0:T(8,128)(2,1)S(1)} %concatenate.41, bf16[1,1024,7168]{2,1,0:T(8,128)(2,1)} %param.31, s32[]{:T(128)S(6)} %select_n.132), kind=kOutput, calls=%fused_computation.41 | convolution fusion | flops 1057480704 | bytes 5292036 | tf_op jit(solution)/shard_map/dot_general | solution.py:218
  129.3 2.6 %collective-permute-done.33 = bf16[288,1792]{1,0:T(8,128)(2,1)S(1)} collective-permute-done((bf16[288,1792]{1,0:T(8,128)(2,1)S(1)}, bf16[288,1792]{1,0:T(8,128)(2,1)S(1)}, u32[]{:S(2)}, u32[]{:S(2)}) %collective-permute-start.33) | collective-permute-done | bytes 1032224 | tf_op jit(solution)/shard_map/ppermute | solution.py:21
  131.9 4.2 %fusion.45 = bf16[288,1792]{1,0:T(8,128)(2,1)} fusion(bf16[288,1024]{1,0:T(8,128)(2,1)S(1)} %concatenate.41, bf16[1,1024,7168]{2,1,0:T(8,128)(2,1)} %param.31, s32[]{:T(128)S(6)} %select_n.131, bf16[288,1792]{1,0:T(8,128)(2,1)S(1)} %collective-permute-done.33), kind=kOutput, calls=%fused_computation.40 | convolution fusion | flops 1058512896 | bytes 6324228 | tf_op jit(solution)/shard_map/dot_general | solution.py:218
  136.1 4.2 %fusion.51 = bf16[288,1792]{1,0:T(8,128)(2,1)} fusion(bf16[288,1024]{1,0:T(8,128)(2,1)S(1)} %concatenate.41, bf16[1,1024,7168]{2,1,0:T(8,128)(2,1)} %param.32, s32[]{:T(128)S(6)} %select_n.132), kind=kOutput, calls=%fused_computation.42 | convolution fusion | flops 1057480704 | bytes 5292036 | tf_op jit(solution)/shard_map/dot_general | solution.py:218
  140.5 4.2 %fusion.60 = bf16[288,1792]{1,0:T(8,128)(2,1)} fusion(bf16[288,1024]{1,0:T(8,128)(2,1)S(1)} %concatenate.41, bf16[1,1024,7168]{2,1,0:T(8,128)(2,1)} %param.31, s32[]{:T(128)S(6)} %select_n.134), kind=kOutput, calls=%fused_computation.45 | convolution fusion | flops 1057480704 | bytes 5292036 | tf_op jit(solution)/shard_map/dot_general | solution.py:218
  145.1 4.3 %fusion.69 = bf16[288,1792]{1,0:T(8,128)(2,1)} fusion(bf16[288,1024]{1,0:T(8,128)(2,1)S(1)} %concatenate.41, bf16[1,1024,7168]{2,1,0:T(8,128)(2,1)} %param.32, s32[]{:T(128)S(6)} %select_n.134), kind=kOutput, calls=%fused_computation.48 | convolution fusion | flops 1057480704 | bytes 5292036 | tf_op jit(solution)/shard_map/dot_general | solution.py:218
  149.6 4.7 %fusion.42 = bf16[288,1792]{1,0:T(8,128)(2,1)} fusion(bf16[288,1024]{1,0:T(8,128)(2,1)} %copy-done.2, bf16[1,1024,7168]{2,1,0:T(8,128)(2,1)} %param.32, s32[]{:T(128)S(6)} %select_n.131, bf16[288,1792]{1,0:T(8,128)(2,1)} %collective-permute-done.34), kind=kOutput, calls=%fused_computation.39 | convolution fusion | flops 1058512896 | bytes 6324228 | tf_op jit(solution)/shard_map/dot_general | solution.py:218
  154.3 1.9 collective-permute-start.38
  156.2 3.5 %fusion.57 = f32[288,1792]{1,0:T(8,128)S(1)} fusion(bf16[288,1024]{1,0:T(8,128)(2,1)} %copy-done.2, bf16[1,1024,7168]{2,1,0:T(8,128)(2,1)} %param.31, s32[]{:T(128)S(6)} %select_n.133), kind=kOutput, calls=%fused_computation.44 | convolution fusion | flops 1057996800 | bytes 6324228 | tf_op jit(solution)/shard_map/dot_general | solution.py:218
  159.8 3.3 %fusion.66 = f32[288,1792]{1,0:T(8,128)S(1)} fusion(bf16[288,1024]{1,0:T(8,128)(2,1)S(1)} %copy-done.3, bf16[1,1024,7168]{2,1,0:T(8,128)(2,1)} %param.32, s32[]{:T(128)S(6)} %select_n.133), kind=kOutput, calls=%fused_computation.47 | convolution fusion | flops 1057996800 | bytes 6324228 | tf_op jit(solution)/shard_map/dot_general | solution.py:218
  163.1 12.3 %collective-permute-done.36 = bf16[288,1792]{1,0:T(8,128)(2,1)S(1)} collective-permute-done((bf16[288,1792]{1,0:T(8,128)(2,1)}, bf16[288,1792]{1,0:T(8,128)(2,1)S(1)}, u32[]{:S(2)}, u32[]{:S(2)}) %collective-permute-start.36) | collective-permute-done | bytes 1032224 | tf_op jit(solution)/shard_map/ppermute | solution.py:21
  175.4 21.6 %collective-permute-done.38 = bf16[288,1792]{1,0:T(8,128)(2,1)} collective-permute-done((bf16[288,1792]{1,0:T(8,128)(2,1)}, bf16[288,1792]{1,0:T(8,128)(2,1)}, u32[]{:S(2)}, u32[]{:S(2)}) %collective-permute-start.38) | collective-permute-done | bytes 1032224 | tf_op jit(solution)/shard_map/ppermute | solution.py:21
  197.0 2.3 multiply_convert_fusion
  199.7 2.3 collective-permute-done.39
  202.0 3.3 %fusion.4 = f32[288,1024]{1,0:T(8,128)S(1)} fusion(bf16[288,1792]{1,0:T(8,128)(2,1)S(1)} %collective-permute-done.39, bf16[1,7168,1024]{2,1,0:T(8,128)(2,1)} %param.33, s32[]{:T(128)S(6)} %select_n.134), kind=kOutput, calls=%fused_computation.5 | convolution fusion | flops 1056964608 | bytes 5881860 | tf_op jit(solution)/shard_map/dot_general | solution.py:240
  205.3 4.4 %fusion.72 = f32[288,1024]{1,0:T(8,128)} fusion(f32[288,1024]{1,0:T(8,128)S(1)} %fusion.4, bf16[288,1792]{1,0:T(8,128)(2,1)S(1)} %multiply_convert_fusion, bf16[1,7168,1024]{2,1,0:T(8,128)(2,1)} %param.33, s32[]{:T(128)S(6)} %select_n.133), kind=kOutput, calls=%fused_computation.51 | convolution fusion | flops 1057259520 | bytes 7061508 | tf_op jit(solution)/shard_map/dot_general | solution.py:240
  209.7 14.9 %collective-permute-done.40 = bf16[288,1792]{1,0:T(8,128)(2,1)S(1)} collective-permute-done((bf16[288,1792]{1,0:T(8,128)(2,1)S(1)}, bf16[288,1792]{1,0:T(8,128)(2,1)S(1)}, u32[]{:S(2)}, u32[]{:S(2)}) %collective-permute-start.40) | collective-permute-done | bytes 1032224 | tf_op jit(solution)/shard_map/ppermute | solution.py:21
  226.3 3.6 %fusion.2 = f32[288,1024]{1,0:T(8,128)S(1)} fusion(bf16[288,1792]{1,0:T(8,128)(2,1)S(1)} %collective-permute-done.40, bf16[1,7168,1024]{2,1,0:T(8,128)(2,1)} %param.33, s32[]{:T(128)S(6)} %select_n.131), kind=kOutput, calls=%fused_computation.3 | convolution fusion | flops 1056964608 | bytes 5881860 | tf_op jit(solution)/shard_map/dot_general | solution.py:240
  230.0 3.3 %add_convert_fusion = bf16[288,1024]{1,0:T(8,128)(2,1)S(1)} fusion(f32[288,1024]{1,0:T(8,128)S(1)} %copy-done.15, f32[288,1024]{1,0:T(8,128)S(1)} %fusion.2, bf16[288,1792]{1,0:T(8,128)(2,1)S(1)} %collective-permute-done.41, bf16[1,7168,1024]{2,1,0:T(8,128)(2,1)} %param.33, s32[]{:T(128)S(6)} %select_n.132), kind=kOutput, calls=%fused_computation.64 | convolution fusion | flops 1057849344 | bytes 7651332 | tf_op jit(solution)/shard_map/dot_general | solution.py:240
  233.4 5.7 %collective-permute-start.42 = (bf16[36,1024]{1,0:T(8,128)(2,1)S(1)}, bf16[36,1024]{1,0:T(8,128)(2,1)S(1)}, u32[]{:S(2)}, u32[]{:S(2)}) collective-permute-start(bf16[36,1024]{1,0:T(8,128)(2,1)S(1)} %get-tuple-element.40), channel_id=1, source_target_pairs={{0,28},{4,0},{8,4},{12,8},{16,12},{20,16},{24,20},{28,24},{1,29},{... | collective-permute-start | bytes 221192 | tf_op jit(solution)/shard_map/ppermute | solution.py:26
  239.5 2.7 %collective-permute-start.45 = (bf16[36,1024]{1,0:T(8,128)(2,1)S(1)}, bf16[36,1024]{1,0:T(8,128)(2,1)S(1)}, u32[]{:S(2)}, u32[]{:S(2)}) collective-permute-start(bf16[36,1024]{1,0:T(8,128)(2,1)S(1)} %get-tuple-element.37), channel_id=1, source_target_pairs={{0,16},{4,20},{8,24},{12,28},{16,0},{20,4},{24,8},{28,12},{1,17},{... | collective-permute-start | bytes 221192 | tf_op jit(solution)/shard_map/ppermute | solution.py:26
  242.4 2.9 %collective-permute-start.47 = (bf16[36,1024]{1,0:T(8,128)(2,1)S(1)}, bf16[36,1024]{1,0:T(8,128)(2,1)S(1)}, u32[]{:S(2)}, u32[]{:S(2)}) collective-permute-start(bf16[36,1024]{1,0:T(8,128)(2,1)S(1)} %get-tuple-element.35), channel_id=1, source_target_pairs={{0,8},{4,12},{8,16},{12,20},{16,24},{20,28},{24,0},{28,4},{1,9},{5... | collective-permute-start | bytes 221192 | tf_op jit(solution)/shard_map/ppermute | solution.py:26
  245.7 8.8 %collective-permute-done.45 = bf16[36,1024]{1,0:T(8,128)(2,1)S(1)} collective-permute-done((bf16[36,1024]{1,0:T(8,128)(2,1)S(1)}, bf16[36,1024]{1,0:T(8,128)(2,1)S(1)}, u32[]{:S(2)}, u32[]{:S(2)}) %collective-permute-start.45) | collective-permute-done | bytes 73760 | tf_op jit(solution)/shard_map/ppermute | solution.py:26
  254.5 1.9 collective-permute-done.46
  (182 shorter events, 40.8 us)
Async XLA Ops:
  2.1 10.6 %collective-permute-start = (bf16[3,1056]{0,1:T(8,128)(2,1)S(1)}, bf16[3,1056]{0,1:T(8,128)(2,1)S(1)}, u32[]{:S(2)}, u32[]{:S(2)}) collective-permute-start(bf16[3,1056]{0,1:T(8,128)(2,1)S(1)} %fusion.122), channel_id=1, source_target_pairs={{0,4},{4,8},{8,12},{12,16},{16,20},{20,24},{24,28},{1,5},{5,9},{9,... | collective-permute-start | bytes 19016 | tf_op jit(solution)/shard_map/ppermute | solution.py:17
  14.8 16.0 %collective-permute-start.1 = (bf16[17,1024]{1,0:T(8,128)(2,1)S(1)}, bf16[17,1024]{1,0:T(8,128)(2,1)S(1)}, u32[]{:S(2)}, u32[]{:S(2)}) collective-permute-start(bf16[17,1024]{1,0:T(8,128)(2,1)S(1)} %pad_maximum_fusion.3), channel_id=1, source_target_pairs={{0,4},{4,8},{8,12},{12,16},{16,20},{20,24},{24,28},{1,5},{5,9},{9,... | collective-permute-start | bytes 104456 | tf_op jit(solution)/shard_map/ppermute | solution.py:17
  19.3 13.1 %collective-permute-start.2 = (bf16[17,1024]{1,0:T(8,128)(2,1)S(1)}, bf16[17,1024]{1,0:T(8,128)(2,1)S(1)}, u32[]{:S(2)}, u32[]{:S(2)}) collective-permute-start(bf16[17,1024]{1,0:T(8,128)(2,1)S(1)} %pad_maximum_fusion.3), channel_id=1, source_target_pairs={{0,8},{4,12},{8,16},{12,20},{16,24},{20,28},{1,9},{5,13},{9,17},{1... | collective-permute-start | bytes 104456 | tf_op jit(solution)/shard_map/ppermute | solution.py:17
  22.8 10.9 %collective-permute-start.3 = (bf16[17,1024]{1,0:T(8,128)(2,1)S(1)}, bf16[17,1024]{1,0:T(8,128)(2,1)S(1)}, u32[]{:S(2)}, u32[]{:S(2)}) collective-permute-start(bf16[17,1024]{1,0:T(8,128)(2,1)S(1)} %pad_maximum_fusion.3), channel_id=1, source_target_pairs={{0,12},{4,16},{8,20},{12,24},{16,28},{1,13},{5,17},{9,21},{13,25},... | collective-permute-start | bytes 104456 | tf_op jit(solution)/shard_map/ppermute | solution.py:17
  28.2 5.6 %collective-permute-start.4 = (bf16[17,1024]{1,0:T(8,128)(2,1)S(1)}, bf16[17,1024]{1,0:T(8,128)(2,1)S(1)}, u32[]{:S(2)}, u32[]{:S(2)}) collective-permute-start(bf16[17,1024]{1,0:T(8,128)(2,1)S(1)} %pad_maximum_fusion.3), channel_id=1, source_target_pairs={{0,16},{4,20},{8,24},{12,28},{1,17},{5,21},{9,25},{13,29},{2,18},{... | collective-permute-start | bytes 104456 | tf_op jit(solution)/shard_map/ppermute | solution.py:17
  29.5 4.3 %collective-permute-start.5 = (bf16[17,1024]{1,0:T(8,128)(2,1)S(1)}, bf16[17,1024]{1,0:T(8,128)(2,1)S(1)}, u32[]{:S(2)}, u32[]{:S(2)}) collective-permute-start(bf16[17,1024]{1,0:T(8,128)(2,1)S(1)} %pad_maximum_fusion.3), channel_id=1, source_target_pairs={{0,20},{4,24},{8,28},{1,21},{5,25},{9,29},{2,22},{6,26},{10,30},{3... | collective-permute-start | bytes 104456 | tf_op jit(solution)/shard_map/ppermute | solution.py:17
  30.8 3.0 %collective-permute-start.6 = (bf16[17,1024]{1,0:T(8,128)(2,1)S(1)}, bf16[17,1024]{1,0:T(8,128)(2,1)S(1)}, u32[]{:S(2)}, u32[]{:S(2)}) collective-permute-start(bf16[17,1024]{1,0:T(8,128)(2,1)S(1)} %pad_maximum_fusion.3), channel_id=1, source_target_pairs={{0,24},{4,28},{1,25},{5,29},{2,26},{6,30},{3,27},{7,31}} | collective-permute-start | bytes 104456 | tf_op jit(solution)/shard_map/ppermute | solution.py:17
  32.4 3.0 %collective-permute-start.7 = (bf16[17,1024]{1,0:T(8,128)(2,1)S(1)}, bf16[17,1024]{1,0:T(8,128)(2,1)S(1)}, u32[]{:S(2)}, u32[]{:S(2)}) collective-permute-start(bf16[17,1024]{1,0:T(8,128)(2,1)S(1)} %pad_maximum_fusion.3), channel_id=1, source_target_pairs={{0,28},{1,29},{2,30},{3,31}} | collective-permute-start | bytes 104456 | tf_op jit(solution)/shard_map/ppermute | solution.py:17
  39.3 11.1 %collective-permute-start.9 = (bf16[128,1024]{1,0:T(8,128)(2,1)S(1)}, bf16[128,1024]{1,0:T(8,128)(2,1)S(1)}, u32[]{:S(2)}, u32[]{:S(2)}) collective-permute-start(bf16[128,1024]{1,0:T(8,128)(2,1)S(1)} %get-tuple-element.33), channel_id=1, source_target_pairs={{0,8},{4,12},{8,16},{12,20},{16,24},{20,28},{24,0},{28,4},{1,9},{5... | collective-permute-start | bytes 786440 | tf_op jit(solution)/shard_map/ppermute | solution.py:26
  39.4 19.0 %collective-permute-start.11 = (bf16[128,1024]{1,0:T(8,128)(2,1)S(1)}, bf16[128,1024]{1,0:T(8,128)(2,1)S(1)}, u32[]{:S(2)}, u32[]{:S(2)}) collective-permute-start(bf16[128,1024]{1,0:T(8,128)(2,1)S(1)} %get-tuple-element.33), channel_id=1, source_target_pairs={{0,16},{4,20},{8,24},{12,28},{16,0},{20,4},{24,8},{28,12},{1,17},{... | collective-permute-start | bytes 786440 | tf_op jit(solution)/shard_map/ppermute | solution.py:26
  42.5 17.7 %collective-permute-start.13 = (bf16[128,1024]{1,0:T(8,128)(2,1)S(1)}, bf16[128,1024]{1,0:T(8,128)(2,1)S(1)}, u32[]{:S(2)}, u32[]{:S(2)}) collective-permute-start(bf16[128,1024]{1,0:T(8,128)(2,1)S(1)} %get-tuple-element.33), channel_id=1, source_target_pairs={{0,24},{4,28},{8,0},{12,4},{16,8},{20,12},{24,16},{28,20},{1,25},{... | collective-permute-start | bytes 786440 | tf_op jit(solution)/shard_map/ppermute | solution.py:26
  43.2 17.2 %collective-permute-start.8 = (bf16[128,1024]{1,0:T(8,128)(2,1)S(1)}, bf16[128,1024]{1,0:T(8,128)(2,1)S(1)}, u32[]{:S(2)}, u32[]{:S(2)}) collective-permute-start(bf16[128,1024]{1,0:T(8,128)(2,1)S(1)} %get-tuple-element.33), channel_id=1, source_target_pairs={{0,4},{4,0},{8,12},{12,8},{16,20},{20,16},{24,28},{28,24},{1,5},{5... | collective-permute-start | bytes 786440 | tf_op jit(solution)/shard_map/ppermute | solution.py:133
  50.4 10.4 %collective-permute-start.10 = (bf16[128,1024]{1,0:T(8,128)(2,1)S(1)}, bf16[128,1024]{1,0:T(8,128)(2,1)S(1)}, u32[]{:S(2)}, u32[]{:S(2)}) collective-permute-start(bf16[128,1024]{1,0:T(8,128)(2,1)S(1)} %collective-permute-done.9), channel_id=1, source_target_pairs={{0,4},{4,0},{8,12},{12,8},{16,20},{20,16},{24,28},{28,24},{1,5},{5... | collective-permute-start | bytes 786440 | tf_op jit(solution)/shard_map/ppermute | solution.py:133
  58.3 9.2 %collective-permute-start.12 = (bf16[128,1024]{1,0:T(8,128)(2,1)S(1)}, bf16[128,1024]{1,0:T(8,128)(2,1)S(1)}, u32[]{:S(2)}, u32[]{:S(2)}) collective-permute-start(bf16[128,1024]{1,0:T(8,128)(2,1)S(1)} %collective-permute-done.11), channel_id=1, source_target_pairs={{0,4},{4,0},{8,12},{12,8},{16,20},{20,16},{24,28},{28,24},{1,5},{5... | collective-permute-start | bytes 786440 | tf_op jit(solution)/shard_map/ppermute | solution.py:133
  60.2 12.0 %collective-permute-start.14 = (bf16[128,1024]{1,0:T(8,128)(2,1)S(1)}, bf16[128,1024]{1,0:T(8,128)(2,1)S(1)}, u32[]{:S(2)}, u32[]{:S(2)}) collective-permute-start(bf16[128,1024]{1,0:T(8,128)(2,1)S(1)} %collective-permute-done.13), channel_id=1, source_target_pairs={{0,4},{4,0},{8,12},{12,8},{16,20},{20,16},{24,28},{28,24},{1,5},{5... | collective-permute-start | bytes 786440 | tf_op jit(solution)/shard_map/ppermute | solution.py:133
  73.8 5.3 %collective-permute-start.15 = (bf16[256,512]{1,0:T(8,128)(2,1)S(1)}, bf16[256,512]{1,0:T(8,128)(2,1)S(1)}, u32[]{:S(2)}, u32[]{:S(2)}) collective-permute-start(bf16[256,512]{1,0:T(8,128)(2,1)S(1)} %get-tuple-element.30), channel_id=1, source_target_pairs={{0,1},{1,0},{2,3},{3,2},{4,5},{5,4},{6,7},{7,6},{8,9},{9,8},{10,11... | collective-permute-start | bytes 786440 | tf_op jit(solution)/shard_map/ppermute | solution.py:21
  75.3 8.6 %collective-permute-start.17 = (bf16[256,512]{1,0:T(8,128)(2,1)}, bf16[256,512]{1,0:T(8,128)(2,1)S(1)}, u32[]{:S(2)}, u32[]{:S(2)}) collective-permute-start(bf16[256,512]{1,0:T(8,128)(2,1)} %fusion.111), channel_id=1, source_target_pairs={{0,2},{1,3},{2,0},{3,1},{4,6},{5,7},{6,4},{7,5},{8,10},{9,11},{10,... | collective-permute-start | bytes 786440 | tf_op jit(solution)/shard_map/ppermute | solution.py:21
  77.2 9.3 %collective-permute-start.20 = (f32[128]{0:T(128)S(1)}, f32[128]{0:T(128)S(1)}, u32[]{:S(2)}, u32[]{:S(2)}) collective-permute-start(f32[128]{0:T(128)S(1)} %get-tuple-element.32), channel_id=1, source_target_pairs={{0,1},{1,0},{2,3},{3,2},{4,5},{5,4},{6,7},{7,6},{8,9},{9,8},{10,11... | collective-permute-start | bytes 1544 | tf_op jit(solution)/shard_map/ppermute | solution.py:21
  77.2 9.2 %collective-permute-start.21 = (f32[128]{0:T(128)S(1)}, f32[128]{0:T(128)S(1)}, u32[]{:S(2)}, u32[]{:S(2)}) collective-permute-start(f32[128]{0:T(128)S(1)} %get-tuple-element.32), channel_id=1, source_target_pairs={{0,2},{1,3},{2,0},{3,1},{4,6},{5,7},{6,4},{7,5},{8,10},{9,11},{10,... | collective-permute-start | bytes 1544 | tf_op jit(solution)/shard_map/ppermute | solution.py:21
  77.8 8.7 %collective-permute-start.22 = (f32[128]{0:T(128)S(1)}, f32[128]{0:T(128)S(1)}, u32[]{:S(2)}, u32[]{:S(2)}) collective-permute-start(f32[128]{0:T(128)S(1)} %get-tuple-element.32), channel_id=1, source_target_pairs={{0,3},{1,2},{2,1},{3,0},{4,7},{5,6},{6,5},{7,4},{8,11},{9,10},{10,... | collective-permute-start | bytes 1544 | tf_op jit(solution)/shard_map/ppermute | solution.py:21
  84.0 2.5 collective-permute-start.18
  84.7 5.0 %collective-permute-start.19 = (bf16[128,512]{1,0:T(8,128)(2,1)S(1)}, bf16[128,512]{1,0:T(8,128)(2,1)S(1)}, u32[]{:S(2)}, u32[]{:S(2)}) collective-permute-start(bf16[128,512]{1,0:T(8,128)(2,1)S(1)} %get-tuple-element.54), channel_id=1, source_target_pairs={{0,4},{1,12},{2,20},{3,28},{4,0},{5,8},{6,16},{7,24},{8,5},{9,13},... | collective-permute-start | bytes 393224 | tf_op jit(solution)/shard_map/ppermute | solution.py:171
  90.0 15.4 %collective-permute-start.23 = (f32[128]{0:T(128)S(1)}, f32[128]{0:T(128)S(1)}, u32[]{:S(2)}, u32[]{:S(2)}) collective-permute-start(f32[128]{0:T(128)S(1)} %fusion.95), channel_id=1, source_target_pairs={{0,1},{1,0},{2,3},{3,2},{4,5},{5,4},{6,7},{7,6},{8,9},{9,8},{10,11... | collective-permute-start | bytes 1544 | tf_op jit(solution)/shard_map/ppermute | solution.py:21
  96.0 10.9 %collective-permute-start.24 = (f32[128]{0:T(128)S(1)}, f32[128]{0:T(128)S(1)}, u32[]{:S(2)}, u32[]{:S(2)}) collective-permute-start(f32[128]{0:T(128)S(1)} %fusion.95), channel_id=1, source_target_pairs={{0,2},{1,3},{2,0},{3,1},{4,6},{5,7},{6,4},{7,5},{8,10},{9,11},{10,... | collective-permute-start | bytes 1544 | tf_op jit(solution)/shard_map/ppermute | solution.py:21
  105.3 3.0 %collective-permute-start.25 = (f32[128]{0:T(128)S(1)}, f32[128]{0:T(128)S(1)}, u32[]{:S(2)}, u32[]{:S(2)}) collective-permute-start(f32[128]{0:T(128)S(1)} %fusion.95), channel_id=1, source_target_pairs={{0,3},{1,2},{2,1},{3,0},{4,7},{5,6},{6,5},{7,4},{8,11},{9,10},{10,... | collective-permute-start | bytes 1544 | tf_op jit(solution)/shard_map/ppermute | solution.py:21
  108.8 8.2 %collective-permute-start.26 = (bf16[36,1024]{1,0:T(8,128)(2,1)S(1)}, bf16[36,1024]{1,0:T(8,128)(2,1)S(1)}, u32[]{:S(2)}, u32[]{:S(2)}) collective-permute-start(bf16[36,1024]{1,0:T(8,128)(2,1)S(1)} %get-tuple-element.47), channel_id=1, source_target_pairs={{0,4},{4,8},{8,12},{12,16},{16,20},{20,24},{24,28},{28,0},{1,5},{5... | collective-permute-start | bytes 221192 | tf_op jit(solution)/shard_map/ppermute | solution.py:26
  109.2 8.0 %collective-permute-start.27 = (bf16[36,1024]{1,0:T(8,128)(2,1)S(1)}, bf16[36,1024]{1,0:T(8,128)(2,1)S(1)}, u32[]{:S(2)}, u32[]{:S(2)}) collective-permute-start(bf16[36,1024]{1,0:T(8,128)(2,1)S(1)} %get-tuple-element.46), channel_id=1, source_target_pairs={{0,8},{4,12},{8,16},{12,20},{16,24},{20,28},{24,0},{28,4},{1,9},{5... | collective-permute-start | bytes 221192 | tf_op jit(solution)/shard_map/ppermute | solution.py:26
  109.8 13.5 %collective-permute-start.28 = (bf16[36,1024]{1,0:T(8,128)(2,1)S(1)}, bf16[36,1024]{1,0:T(8,128)(2,1)S(1)}, u32[]{:S(2)}, u32[]{:S(2)}) collective-permute-start(bf16[36,1024]{1,0:T(8,128)(2,1)S(1)} %get-tuple-element.45), channel_id=1, source_target_pairs={{0,12},{4,16},{8,20},{12,24},{16,28},{20,0},{24,4},{28,8},{1,13},{... | collective-permute-start | bytes 221192 | tf_op jit(solution)/shard_map/ppermute | solution.py:26
  110.5 12.8 %collective-permute-start.29 = (bf16[36,1024]{1,0:T(8,128)(2,1)S(1)}, bf16[36,1024]{1,0:T(8,128)(2,1)S(1)}, u32[]{:S(2)}, u32[]{:S(2)}) collective-permute-start(bf16[36,1024]{1,0:T(8,128)(2,1)S(1)} %get-tuple-element.44), channel_id=1, source_target_pairs={{0,16},{4,20},{8,24},{12,28},{16,0},{20,4},{24,8},{28,12},{1,17},{... | collective-permute-start | bytes 221192 | tf_op jit(solution)/shard_map/ppermute | solution.py:26
  114.8 8.5 %collective-permute-start.30 = (bf16[36,1024]{1,0:T(8,128)(2,1)S(1)}, bf16[36,1024]{1,0:T(8,128)(2,1)S(1)}, u32[]{:S(2)}, u32[]{:S(2)}) collective-permute-start(bf16[36,1024]{1,0:T(8,128)(2,1)S(1)} %get-tuple-element.43), channel_id=1, source_target_pairs={{0,20},{4,24},{8,28},{12,0},{16,4},{20,8},{24,12},{28,16},{1,21},{... | collective-permute-start | bytes 221192 | tf_op jit(solution)/shard_map/ppermute | solution.py:26
  117.0 7.8 %collective-permute-start.31 = (bf16[36,1024]{1,0:T(8,128)(2,1)S(1)}, bf16[36,1024]{1,0:T(8,128)(2,1)S(1)}, u32[]{:S(2)}, u32[]{:S(2)}) collective-permute-start(bf16[36,1024]{1,0:T(8,128)(2,1)S(1)} %get-tuple-element.42), channel_id=1, source_target_pairs={{0,24},{4,28},{8,0},{12,4},{16,8},{20,12},{24,16},{28,20},{1,25},{... | collective-permute-start | bytes 221192 | tf_op jit(solution)/shard_map/ppermute | solution.py:26
  117.2 7.6 %collective-permute-start.32 = (bf16[36,1024]{1,0:T(8,128)(2,1)S(1)}, bf16[36,1024]{1,0:T(8,128)(2,1)S(1)}, u32[]{:S(2)}, u32[]{:S(2)}) collective-permute-start(bf16[36,1024]{1,0:T(8,128)(2,1)S(1)} %get-tuple-element.41), channel_id=1, source_target_pairs={{0,28},{4,0},{8,4},{12,8},{16,12},{20,16},{24,20},{28,24},{1,29},{... | collective-permute-start | bytes 221192 | tf_op jit(solution)/shard_map/ppermute | solution.py:26
  129.2 2.7 %collective-permute-start.33 = (bf16[288,1792]{1,0:T(8,128)(2,1)S(1)}, bf16[288,1792]{1,0:T(8,128)(2,1)S(1)}, u32[]{:S(2)}, u32[]{:S(2)}) collective-permute-start(bf16[288,1792]{1,0:T(8,128)(2,1)S(1)} %fusion.48), channel_id=1, source_target_pairs={{0,1},{1,0},{2,3},{3,2},{4,5},{5,4},{6,7},{7,6},{8,9},{9,8},{10,11... | collective-permute-start | bytes 3096584 | tf_op jit(solution)/shard_map/ppermute | solution.py:21
  140.4 9.2 %collective-permute-start.34 = (bf16[288,1792]{1,0:T(8,128)(2,1)}, bf16[288,1792]{1,0:T(8,128)(2,1)}, u32[]{:S(2)}, u32[]{:S(2)}) collective-permute-start(bf16[288,1792]{1,0:T(8,128)(2,1)} %fusion.51), channel_id=1, source_target_pairs={{0,1},{1,0},{2,3},{3,2},{4,5},{5,4},{6,7},{7,6},{8,9},{9,8},{10,11... | collective-permute-start | bytes 3096584 | tf_op jit(solution)/shard_map/ppermute | solution.py:21
  144.7 18.3 %collective-permute-start.35 = (bf16[288,1792]{1,0:T(8,128)(2,1)}, bf16[288,1792]{1,0:T(8,128)(2,1)S(1)}, u32[]{:S(2)}, u32[]{:S(2)}) collective-permute-start(bf16[288,1792]{1,0:T(8,128)(2,1)} %fusion.60), channel_id=1, source_target_pairs={{0,1},{1,0},{2,3},{3,2},{4,5},{5,4},{6,7},{7,6},{8,9},{9,8},{10,11... | collective-permute-start | bytes 3096584 | tf_op jit(solution)/shard_map/ppermute | solution.py:21
  149.4 13.7 %collective-permute-start.37 = (bf16[288,1792]{1,0:T(8,128)(2,1)}, bf16[288,1792]{1,0:T(8,128)(2,1)S(1)}, u32[]{:S(2)}, u32[]{:S(2)}) collective-permute-start(bf16[288,1792]{1,0:T(8,128)(2,1)} %fusion.69), channel_id=1, source_target_pairs={{0,1},{1,0},{2,3},{3,2},{4,5},{5,4},{6,7},{7,6},{8,9},{9,8},{10,11... | collective-permute-start | bytes 3096584 | tf_op jit(solution)/shard_map/ppermute | solution.py:21
  149.5 25.9 %collective-permute-start.36 = (bf16[288,1792]{1,0:T(8,128)(2,1)}, bf16[288,1792]{1,0:T(8,128)(2,1)S(1)}, u32[]{:S(2)}, u32[]{:S(2)}) collective-permute-start(bf16[288,1792]{1,0:T(8,128)(2,1)} %fusion.45), channel_id=1, source_target_pairs={{0,2},{1,3},{2,0},{3,1},{4,6},{5,7},{6,4},{7,5},{8,10},{9,11},{10,... | collective-permute-start | bytes 3096584 | tf_op jit(solution)/shard_map/ppermute | solution.py:21
  154.3 42.7 %collective-permute-start.38 = (bf16[288,1792]{1,0:T(8,128)(2,1)}, bf16[288,1792]{1,0:T(8,128)(2,1)}, u32[]{:S(2)}, u32[]{:S(2)}) collective-permute-start(bf16[288,1792]{1,0:T(8,128)(2,1)} %fusion.42), channel_id=1, source_target_pairs={{0,2},{1,3},{2,0},{3,1},{4,6},{5,7},{6,4},{7,5},{8,10},{9,11},{10,... | collective-permute-start | bytes 3096584 | tf_op jit(solution)/shard_map/ppermute | solution.py:21
  199.3 2.7 %collective-permute-start.39 = (bf16[288,1792]{1,0:T(8,128)(2,1)S(1)}, bf16[288,1792]{1,0:T(8,128)(2,1)S(1)}, u32[]{:S(2)}, u32[]{:S(2)}) collective-permute-start(bf16[288,1792]{1,0:T(8,128)(2,1)S(1)} %multiply_convert_fusion), channel_id=1, source_target_pairs={{0,1},{1,0},{2,3},{3,2},{4,5},{5,4},{6,7},{7,6},{8,9},{9,8},{10,11... | collective-permute-start | bytes 3096584 | tf_op jit(solution)/shard_map/ppermute | solution.py:21
  199.4 25.2 %collective-permute-start.40 = (bf16[288,1792]{1,0:T(8,128)(2,1)S(1)}, bf16[288,1792]{1,0:T(8,128)(2,1)S(1)}, u32[]{:S(2)}, u32[]{:S(2)}) collective-permute-start(bf16[288,1792]{1,0:T(8,128)(2,1)S(1)} %multiply_convert_fusion), channel_id=1, source_target_pairs={{0,2},{1,3},{2,0},{3,1},{4,6},{5,7},{6,4},{7,5},{8,10},{9,11},{10,... | collective-permute-start | bytes 3096584 | tf_op jit(solution)/shard_map/ppermute | solution.py:21
  224.6 5.4 %collective-permute-start.41 = (bf16[288,1792]{1,0:T(8,128)(2,1)S(1)}, bf16[288,1792]{1,0:T(8,128)(2,1)S(1)}, u32[]{:S(2)}, u32[]{:S(2)}) collective-permute-start(bf16[288,1792]{1,0:T(8,128)(2,1)S(1)} %collective-permute-done.40), channel_id=1, source_target_pairs={{0,1},{1,0},{2,3},{3,2},{4,5},{5,4},{6,7},{7,6},{8,9},{9,8},{10,11... | collective-permute-start | bytes 3096584 | tf_op jit(solution)/shard_map/ppermute | solution.py:21
  233.4 9.0 %collective-permute-start.42 = (bf16[36,1024]{1,0:T(8,128)(2,1)S(1)}, bf16[36,1024]{1,0:T(8,128)(2,1)S(1)}, u32[]{:S(2)}, u32[]{:S(2)}) collective-permute-start(bf16[36,1024]{1,0:T(8,128)(2,1)S(1)} %get-tuple-element.40), channel_id=1, source_target_pairs={{0,28},{4,0},{8,4},{12,8},{16,12},{20,16},{24,20},{28,24},{1,29},{... | collective-permute-start | bytes 221192 | tf_op jit(solution)/shard_map/ppermute | solution.py:26
  239.2 6.1 %collective-permute-start.43 = (bf16[36,1024]{1,0:T(8,128)(2,1)S(1)}, bf16[36,1024]{1,0:T(8,128)(2,1)S(1)}, u32[]{:S(2)}, u32[]{:S(2)}) collective-permute-start(bf16[36,1024]{1,0:T(8,128)(2,1)S(1)} %get-tuple-element.39), channel_id=1, source_target_pairs={{0,24},{4,28},{8,0},{12,4},{16,8},{20,12},{24,16},{28,20},{1,25},{... | collective-permute-start | bytes 221192 | tf_op jit(solution)/shard_map/ppermute | solution.py:26
  239.2 6.5 %collective-permute-start.44 = (bf16[36,1024]{1,0:T(8,128)(2,1)S(1)}, bf16[36,1024]{1,0:T(8,128)(2,1)S(1)}, u32[]{:S(2)}, u32[]{:S(2)}) collective-permute-start(bf16[36,1024]{1,0:T(8,128)(2,1)S(1)} %get-tuple-element.38), channel_id=1, source_target_pairs={{0,20},{4,24},{8,28},{12,0},{16,4},{20,8},{24,12},{28,16},{1,21},{... | collective-permute-start | bytes 221192 | tf_op jit(solution)/shard_map/ppermute | solution.py:26
  239.5 15.0 %collective-permute-start.45 = (bf16[36,1024]{1,0:T(8,128)(2,1)S(1)}, bf16[36,1024]{1,0:T(8,128)(2,1)S(1)}, u32[]{:S(2)}, u32[]{:S(2)}) collective-permute-start(bf16[36,1024]{1,0:T(8,128)(2,1)S(1)} %get-tuple-element.37), channel_id=1, source_target_pairs={{0,16},{4,20},{8,24},{12,28},{16,0},{20,4},{24,8},{28,12},{1,17},{... | collective-permute-start | bytes 221192 | tf_op jit(solution)/shard_map/ppermute | solution.py:26
  242.2 14.2 %collective-permute-start.46 = (bf16[36,1024]{1,0:T(8,128)(2,1)S(1)}, bf16[36,1024]{1,0:T(8,128)(2,1)S(1)}, u32[]{:S(2)}, u32[]{:S(2)}) collective-permute-start(bf16[36,1024]{1,0:T(8,128)(2,1)S(1)} %get-tuple-element.36), channel_id=1, source_target_pairs={{0,12},{4,16},{8,20},{12,24},{16,28},{20,0},{24,4},{28,8},{1,13},{... | collective-permute-start | bytes 221192 | tf_op jit(solution)/shard_map/ppermute | solution.py:26
  242.4 14.0 %collective-permute-start.47 = (bf16[36,1024]{1,0:T(8,128)(2,1)S(1)}, bf16[36,1024]{1,0:T(8,128)(2,1)S(1)}, u32[]{:S(2)}, u32[]{:S(2)}) collective-permute-start(bf16[36,1024]{1,0:T(8,128)(2,1)S(1)} %get-tuple-element.35), channel_id=1, source_target_pairs={{0,8},{4,12},{8,16},{12,20},{16,24},{20,28},{24,0},{28,4},{1,9},{5... | collective-permute-start | bytes 221192 | tf_op jit(solution)/shard_map/ppermute | solution.py:26
  245.2 11.1 %collective-permute-start.48 = (bf16[36,1024]{1,0:T(8,128)(2,1)S(1)}, bf16[36,1024]{1,0:T(8,128)(2,1)S(1)}, u32[]{:S(2)}, u32[]{:S(2)}) collective-permute-start(bf16[36,1024]{1,0:T(8,128)(2,1)S(1)} %get-tuple-element.34), channel_id=1, source_target_pairs={{0,4},{4,8},{8,12},{12,16},{16,20},{20,24},{24,28},{28,0},{1,5},{5... | collective-permute-start | bytes 221192 | tf_op jit(solution)/shard_map/ppermute | solution.py:26
  (17 other events, 228.2 us)
where the time goes:
time: 262 us; the launch traced here: 261 us
  waiting for transfers between devices  109 us (42%)
  starting transfers between devices  78.9 us (30%)
  matrix products  52.7 us (20%)
  other arithmetic  11.4 us (4%)
  local copies, waits for them, and re-layouts  8.35 us (3%)
    ppermute x18, waiting for transfers between devices, swapped(): lax.ppermute(value, 'tp', [(p, p ^ distance) for p in range(lax.axis_size...  61.6 us
    dot_general x8, matrix products, product(): return jnp.dot(source, columns, preferred_element_type=jnp.float32)  31.9 us
    ppermute x17, waiting for transfers between devices, rotated(): lax.ppermute(value, 'ctx', [(c, (c + steps) % count) for c in range(count)])  28.9 us
    ppermute x17, starting transfers between devices, rotated(): lax.ppermute(value, 'ctx', [(c, (c + steps) % count) for c in range(count)])  24.5 us
    ppermute x8, starting transfers between devices, passed_along(): lax.ppermute(value, axis, [(source, source + steps) for source in range(f...  23.3 us
    ppermute x18, starting transfers between devices, swapped(): lax.ppermute(value, 'tp', [(p, p ^ distance) for p in range(lax.axis_size...  22.6 us
    dot_general x4, matrix products, lowered(): return jnp.dot(part, rows, preferred_element_type=jnp.float32)  14.6 us
    ppermute x4, waiting for transfers between devices, body(): lax.ppermute(block, 'ctx', [(c, c ^ 1) for c in range(context_count)])  10.5 us
  transfers between devices with their start and end apart: 49, of which 21 were waited for; matrix products, arithmetic and copies ran while one was open for 15% of the time, Pallas kernels for 0%

commit v1 on v0

--- a/solution.py
+++ b/solution.py
@@ -232,21 +232,27 @@
         for weight, near, far in zip((gate_local, up_local), nears, fars)
     )
     share = (jax.nn.silu(gate_share) * up_share).astype(jnp.bfloat16)
-    share_across = swapped(share, 2)
+    half = hidden // 2
+    arriving = [swapped(share[:, :half], 2)]
+    arriving.append(swapped(share[:, half:], 2))
     share_beside = swapped(share, 1)
 
-    def lowered(part, quarter):
-        rows = lax.dynamic_slice_in_dim(down_local, quarter * hidden, hidden, 0)
+    def lowered(part, quarter, skipped=0):
+        rows = lax.dynamic_slice_in_dim(
+            down_local, quarter * hidden + skipped, part.shape[1], 0
+        )
         return jnp.dot(part, rows, preferred_element_type=jnp.float32)
 
-    local = lowered(share, own) + lowered(share_beside, beside)
-    local, share_across = lax.optimization_barrier((local, share_across))
-    share_diagonal = swapped(share_across, 1)
-    answer = (
-        local
-        + lowered(share_across, across)
-        + lowered(share_diagonal, diagonal)
-    ).astype(jnp.bfloat16)
+    answer = lowered(share, own) + lowered(share_beside, beside)
+    for k, part in enumerate(arriving):
+        answer, part = lax.optimization_barrier((answer, part))
+        forwarded = swapped(part, 1)
+        answer = (
+            answer
+            + lowered(part, across, k * half)
+            + lowered(forwarded, diagonal, k * half)
+        )
+    answer = answer.astype(jnp.bfloat16)
     answer = answer.reshape(sources, items, depth)
     if direct:
         answers = jnp.stack(

time: 262 us -> 265 us (1.011)
    dot_general x4 -> x6, matrix products: 14.6 us -> 16.4 us  [lowered(): return jnp.dot(part, rows, preferred_element_type=jnp.float32)]
    ppermute x18 -> x20, waiting for transfers between devices: 61.6 us -> 60.8 us  [swapped(): lax.ppermute(value, 'tp', [(p, p ^ distance) for p in range(lax.axis_size...]
    ppermute x18 -> x20, starting transfers between devices: 22.6 us -> 22.8 us  [swapped(): lax.ppermute(value, 'tp', [(p, p ^ distance) for p in range(lax.axis_size...]
  transfers between devices with their start and end apart: 49 -> 51, of which waited for: 21 -> 22; matrix products, arithmetic and copies ran while one was open for 15% -> 17% of each run, Pallas kernels for 0% -> 0%
where the time goes in v1:
time: 265 us; the launch traced here: 264 us
  waiting for transfers between devices  108 us (41%)
  starting transfers between devices  79.2 us (30%)
  matrix products  54.5 us (21%)
  other arithmetic  12.5 us (5%)
  local copies, waits for them, and re-layouts  9.12 us (3%)
    ppermute x20, waiting for transfers between devices, swapped(): lax.ppermute(value, 'tp', [(p, p ^ distance) for p in range(lax.axis_size...  60.8 us
    dot_general x8, matrix products, product(): return jnp.dot(source, columns, preferred_element_type=jnp.float32)  31.9 us
    ppermute x17, waiting for transfers between devices, rotated(): lax.ppermute(value, 'ctx', [(c, (c + steps) % count) for c in range(count)])  28.9 us
    ppermute x17, starting transfers between devices, rotated(): lax.ppermute(value, 'ctx', [(c, (c + steps) % count) for c in range(count)])  24.5 us
    ppermute x8, starting transfers between devices, passed_along(): lax.ppermute(value, axis, [(source, source + steps) for source in range(f...  23.3 us
    ppermute x20, starting transfers between devices, swapped(): lax.ppermute(value, 'tp', [(p, p ^ distance) for p in range(lax.axis_size...  22.8 us
    dot_general x6, matrix products, lowered(): return jnp.dot(part, rows, preferred_element_type=jnp.float32)  16.4 us
    ppermute x4, waiting for transfers between devices, body(): lax.ppermute(block, 'ctx', [(c, c ^ 1) for c in range(context_count)])  10.5 us
  transfers between devices with their start and end apart: 51, of which 22 were waited for; matrix products, arithmetic and copies ran while one was open for 17% of the time, Pallas kernels for 0%

profile of v1, /device:TPU:0, one launch (start us, length us, event | category | flops | bytes accessed | tf_op | source)
XLA Modules:
  0.0 264.0 jit_solution(5629104521680218004)
XLA Ops:
  2.1 4.9 %collective-permute-start = (bf16[3,1056]{0,1:T(8,128)(2,1)S(1)}, bf16[3,1056]{0,1:T(8,128)(2,1)S(1)}, u32[]{:S(2)}, u32[]{:S(2)}) collective-permute-start(bf16[3,1056]{0,1:T(8,128)(2,1)S(1)} %fusion.128), channel_id=1, source_target_pairs={{0,4},{4,8},{8,12},{12,16},{16,20},{20,24},{24,28},{1,5},{5,9},{9,... | collective-permute-start | bytes 19016 | tf_op jit(solution)/shard_map/ppermute | solution.py:17
  9.9 2.8 %collective-permute-done = bf16[3,1056]{0,1:T(8,128)(2,1)S(1)} collective-permute-done((bf16[3,1056]{0,1:T(8,128)(2,1)S(1)}, bf16[3,1056]{0,1:T(8,128)(2,1)S(1)}, u32[]{:S(2)}, u32[]{:S(2)}) %collective-permute-start) | collective-permute-done | bytes 6368 | tf_op jit(solution)/shard_map/ppermute | solution.py:17
  14.8 4.4 %collective-permute-start.1 = (bf16[17,1024]{1,0:T(8,128)(2,1)S(1)}, bf16[17,1024]{1,0:T(8,128)(2,1)S(1)}, u32[]{:S(2)}, u32[]{:S(2)}) collective-permute-start(bf16[17,1024]{1,0:T(8,128)(2,1)S(1)} %pad_maximum_fusion.3), channel_id=1, source_target_pairs={{0,4},{4,8},{8,12},{12,16},{16,20},{20,24},{24,28},{1,5},{5,9},{9,... | collective-permute-start | bytes 104456 | tf_op jit(solution)/shard_map/ppermute | solution.py:17
  19.3 3.5 %collective-permute-start.2 = (bf16[17,1024]{1,0:T(8,128)(2,1)S(1)}, bf16[17,1024]{1,0:T(8,128)(2,1)S(1)}, u32[]{:S(2)}, u32[]{:S(2)}) collective-permute-start(bf16[17,1024]{1,0:T(8,128)(2,1)S(1)} %pad_maximum_fusion.3), channel_id=1, source_target_pairs={{0,8},{4,12},{8,16},{12,20},{16,24},{20,28},{1,9},{5,13},{9,17},{1... | collective-permute-start | bytes 104456 | tf_op jit(solution)/shard_map/ppermute | solution.py:17
  22.8 5.4 %collective-permute-start.3 = (bf16[17,1024]{1,0:T(8,128)(2,1)S(1)}, bf16[17,1024]{1,0:T(8,128)(2,1)S(1)}, u32[]{:S(2)}, u32[]{:S(2)}) collective-permute-start(bf16[17,1024]{1,0:T(8,128)(2,1)S(1)} %pad_maximum_fusion.3), channel_id=1, source_target_pairs={{0,12},{4,16},{8,20},{12,24},{16,28},{1,13},{5,17},{9,21},{13,25},... | collective-permute-start | bytes 104456 | tf_op jit(solution)/shard_map/ppermute | solution.py:17
  36.5 2.2 fusion.82
  39.4 3.1 %collective-permute-start.11 = (bf16[128,1024]{1,0:T(8,128)(2,1)S(1)}, bf16[128,1024]{1,0:T(8,128)(2,1)S(1)}, u32[]{:S(2)}, u32[]{:S(2)}) collective-permute-start(bf16[128,1024]{1,0:T(8,128)(2,1)S(1)} %get-tuple-element.39), channel_id=1, source_target_pairs={{0,16},{4,20},{8,24},{12,28},{16,0},{20,4},{24,8},{28,12},{1,17},{... | collective-permute-start | bytes 786440 | tf_op jit(solution)/shard_map/ppermute | solution.py:26
  43.2 2.4 collective-permute-start.8
  45.5 4.9 %collective-permute-done.9 = bf16[128,1024]{1,0:T(8,128)(2,1)S(1)} collective-permute-done((bf16[128,1024]{1,0:T(8,128)(2,1)S(1)}, bf16[128,1024]{1,0:T(8,128)(2,1)S(1)}, u32[]{:S(2)}, u32[]{:S(2)}) %collective-permute-start.9) | collective-permute-done | bytes 262176 | tf_op jit(solution)/shard_map/ppermute | solution.py:26
  52.5 5.8 %collective-permute-done.11 = bf16[128,1024]{1,0:T(8,128)(2,1)S(1)} collective-permute-done((bf16[128,1024]{1,0:T(8,128)(2,1)S(1)}, bf16[128,1024]{1,0:T(8,128)(2,1)S(1)}, u32[]{:S(2)}, u32[]{:S(2)}) %collective-permute-start.11) | collective-permute-done | bytes 262176 | tf_op jit(solution)/shard_map/ppermute | solution.py:26
  58.3 1.8 collective-permute-start.12
  61.3 6.3 %collective-permute-done.12 = bf16[128,1024]{1,0:T(8,128)(2,1)S(1)} collective-permute-done((bf16[128,1024]{1,0:T(8,128)(2,1)S(1)}, bf16[128,1024]{1,0:T(8,128)(2,1)S(1)}, u32[]{:S(2)}, u32[]{:S(2)}) %collective-permute-start.12) | collective-permute-done | bytes 262176 | tf_op jit(solution)/shard_map/ppermute | solution.py:133
  68.0 4.2 %collective-permute-done.14 = bf16[128,1024]{1,0:T(8,128)(2,1)S(1)} collective-permute-done((bf16[128,1024]{1,0:T(8,128)(2,1)S(1)}, bf16[128,1024]{1,0:T(8,128)(2,1)S(1)}, u32[]{:S(2)}, u32[]{:S(2)}) %collective-permute-start.14) | collective-permute-done | bytes 262176 | tf_op jit(solution)/shard_map/ppermute | solution.py:133
  79.5 4.5 %collective-permute-done.17 = bf16[256,512]{1,0:T(8,128)(2,1)S(1)} collective-permute-done((bf16[256,512]{1,0:T(8,128)(2,1)S(1)}, bf16[256,512]{1,0:T(8,128)(2,1)S(1)}, u32[]{:S(2)}, u32[]{:S(2)}) %collective-permute-start.17) | collective-permute-done | bytes 262176 | tf_op jit(solution)/shard_map/ppermute | solution.py:21
  86.8 3.2 %collective-permute-done.19 = bf16[128,512]{1,0:T(8,128)(2,1)S(1)} collective-permute-done((bf16[128,512]{1,0:T(8,128)(2,1)S(1)}, bf16[128,512]{1,0:T(8,128)(2,1)S(1)}, u32[]{:S(2)}, u32[]{:S(2)}) %collective-permute-start.19) | collective-permute-done | bytes 131104 | tf_op jit(solution)/shard_map/ppermute | solution.py:171
  90.3 5.9 %collective-permute-start.23 = (f32[128]{0:T(128)S(1)}, f32[128]{0:T(128)S(1)}, u32[]{:S(2)}, u32[]{:S(2)}) collective-permute-start(f32[128]{0:T(128)S(1)} %fusion.101), channel_id=1, source_target_pairs={{0,1},{1,0},{2,3},{3,2},{4,5},{5,4},{6,7},{7,6},{8,9},{9,8},{10,11... | collective-permute-start | bytes 1544 | tf_op jit(solution)/shard_map/ppermute | solution.py:21
  96.2 9.4 %collective-permute-start.24 = (f32[128]{0:T(128)S(1)}, f32[128]{0:T(128)S(1)}, u32[]{:S(2)}, u32[]{:S(2)}) collective-permute-start(f32[128]{0:T(128)S(1)} %fusion.101), channel_id=1, source_target_pairs={{0,2},{1,3},{2,0},{3,1},{4,6},{5,7},{6,4},{7,5},{8,10},{9,11},{10,... | collective-permute-start | bytes 1544 | tf_op jit(solution)/shard_map/ppermute | solution.py:21
  110.7 4.3 %collective-permute-start.29 = (bf16[36,1024]{1,0:T(8,128)(2,1)S(1)}, bf16[36,1024]{1,0:T(8,128)(2,1)S(1)}, u32[]{:S(2)}, u32[]{:S(2)}) collective-permute-start(bf16[36,1024]{1,0:T(8,128)(2,1)S(1)} %get-tuple-element.50), channel_id=1, source_target_pairs={{0,16},{4,20},{8,24},{12,28},{16,0},{20,4},{24,8},{28,12},{1,17},{... | collective-permute-start | bytes 221192 | tf_op jit(solution)/shard_map/ppermute | solution.py:26
  115.1 2.2 collective-permute-done.26
  117.4 2.3 collective-permute-start.32
  119.7 3.8 %collective-permute-done.28 = bf16[36,1024]{1,0:T(8,128)(2,1)S(1)} collective-permute-done((bf16[36,1024]{1,0:T(8,128)(2,1)S(1)}, bf16[36,1024]{1,0:T(8,128)(2,1)S(1)}, u32[]{:S(2)}, u32[]{:S(2)}) %collective-permute-start.28) | collective-permute-done | bytes 73760 | tf_op jit(solution)/shard_map/ppermute | solution.py:26
  125.9 3.5 %fusion.42 = bf16[288,1792]{1,0:T(8,128)(2,1)S(1)} fusion(bf16[288,1024]{1,0:T(8,128)(2,1)S(1)} %concatenate.41, bf16[1,1024,7168]{2,1,0:T(8,128)(2,1)} %param.31, s32[]{:T(128)S(6)} %select_n.138), kind=kOutput, calls=%fused_computation.35 | convolution fusion | flops 1057480704 | bytes 5292036 | tf_op jit(solution)/shard_map/dot_general | solution.py:218
  129.5 2.6 collective-permute-done.33
  132.1 4.2 %fusion.39 = bf16[288,1792]{1,0:T(8,128)(2,1)} fusion(bf16[288,1024]{1,0:T(8,128)(2,1)S(1)} %concatenate.41, bf16[1,1024,7168]{2,1,0:T(8,128)(2,1)} %param.31, s32[]{:T(128)S(6)} %select_n.137, bf16[288,1792]{1,0:T(8,128)(2,1)S(1)} %collective-permute-done.33), kind=kOutput, calls=%fused_computation.34 | convolution fusion | flops 1058512896 | bytes 6324228 | tf_op jit(solution)/shard_map/dot_general | solution.py:218
  136.4 4.2 %fusion.45 = bf16[288,1792]{1,0:T(8,128)(2,1)} fusion(bf16[288,1024]{1,0:T(8,128)(2,1)S(1)} %concatenate.41, bf16[1,1024,7168]{2,1,0:T(8,128)(2,1)} %param.32, s32[]{:T(128)S(6)} %select_n.138), kind=kOutput, calls=%fused_computation.36 | convolution fusion | flops 1057480704 | bytes 5292036 | tf_op jit(solution)/shard_map/dot_general | solution.py:218
  140.7 4.2 %fusion.54 = bf16[288,1792]{1,0:T(8,128)(2,1)} fusion(bf16[288,1024]{1,0:T(8,128)(2,1)S(1)} %concatenate.41, bf16[1,1024,7168]{2,1,0:T(8,128)(2,1)} %param.31, s32[]{:T(128)S(6)} %select_n.140), kind=kOutput, calls=%fused_computation.39 | convolution fusion | flops 1057480704 | bytes 5292036 | tf_op jit(solution)/shard_map/dot_general | solution.py:218
  145.4 4.3 %fusion.63 = bf16[288,1792]{1,0:T(8,128)(2,1)} fusion(bf16[288,1024]{1,0:T(8,128)(2,1)S(1)} %concatenate.41, bf16[1,1024,7168]{2,1,0:T(8,128)(2,1)} %param.32, s32[]{:T(128)S(6)} %select_n.140), kind=kOutput, calls=%fused_computation.42 | convolution fusion | flops 1057480704 | bytes 5292036 | tf_op jit(solution)/shard_map/dot_general | solution.py:218
  149.9 4.7 %fusion.36 = bf16[288,1792]{1,0:T(8,128)(2,1)} fusion(bf16[288,1024]{1,0:T(8,128)(2,1)} %copy-done.2, bf16[1,1024,7168]{2,1,0:T(8,128)(2,1)} %param.32, s32[]{:T(128)S(6)} %select_n.137, bf16[288,1792]{1,0:T(8,128)(2,1)} %collective-permute-done.34), kind=kOutput, calls=%fused_computation.33 | convolution fusion | flops 1058512896 | bytes 6324228 | tf_op jit(solution)/shard_map/dot_general | solution.py:218
  154.6 1.9 collective-permute-start.38
  156.5 3.5 %fusion.51 = f32[288,1792]{1,0:T(8,128)S(1)} fusion(bf16[288,1024]{1,0:T(8,128)(2,1)} %copy-done.2, bf16[1,1024,7168]{2,1,0:T(8,128)(2,1)} %param.31, s32[]{:T(128)S(6)} %select_n.139), kind=kOutput, calls=%fused_computation.38 | convolution fusion | flops 1057996800 | bytes 6324228 | tf_op jit(solution)/shard_map/dot_general | solution.py:218
  160.0 3.3 %fusion.60 = f32[288,1792]{1,0:T(8,128)S(1)} fusion(bf16[288,1024]{1,0:T(8,128)(2,1)S(1)} %copy-done.3, bf16[1,1024,7168]{2,1,0:T(8,128)(2,1)} %param.32, s32[]{:T(128)S(6)} %select_n.139), kind=kOutput, calls=%fused_computation.41 | convolution fusion | flops 1057996800 | bytes 6324228 | tf_op jit(solution)/shard_map/dot_general | solution.py:218
  163.3 12.3 %collective-permute-done.36 = bf16[288,1792]{1,0:T(8,128)(2,1)S(1)} collective-permute-done((bf16[288,1792]{1,0:T(8,128)(2,1)}, bf16[288,1792]{1,0:T(8,128)(2,1)S(1)}, u32[]{:S(2)}, u32[]{:S(2)}) %collective-permute-start.36) | collective-permute-done | bytes 1032224 | tf_op jit(solution)/shard_map/ppermute | solution.py:21
  175.6 21.6 %collective-permute-done.38 = bf16[288,1792]{1,0:T(8,128)(2,1)} collective-permute-done((bf16[288,1792]{1,0:T(8,128)(2,1)}, bf16[288,1792]{1,0:T(8,128)(2,1)}, u32[]{:S(2)}, u32[]{:S(2)}) %collective-permute-start.38) | collective-permute-done | bytes 1032224 | tf_op jit(solution)/shard_map/ppermute | solution.py:21
  197.3 2.3 multiply_convert_fusion
  202.2 3.3 %fusion = f32[288,1024]{1,0:T(8,128)S(1)} fusion(bf16[288,1792]{1,0:T(8,128)(2,1)S(1)} %collective-permute-done.39, bf16[1,7168,1024]{2,1,0:T(8,128)(2,1)} %param.33, s32[]{:T(128)S(6)} %select_n.140), kind=kOutput, calls=%fused_computation.1 | convolution fusion | flops 1056964608 | bytes 5881860 | tf_op jit(solution)/shard_map/dot_general | solution.py:244
  205.6 3.3 %fusion.78 = f32[288,1024]{1,0:T(8,128)S(1)} fusion(f32[288,1024]{1,0:T(8,128)S(1)} %fusion, bf16[288,1792]{1,0:T(8,128)(2,1)S(1)} %multiply_convert_fusion, bf16[1,7168,1024]{2,1,0:T(8,128)(2,1)} %param.33, s32[]{:T(128)S(6)} %select_n.139), kind=kOutput, calls=%fused_computation.57 | convolution fusion | flops 1057259520 | bytes 7061508 | tf_op jit(solution)/shard_map/dot_general | solution.py:244
  208.9 5.7 %collective-permute-done.40 = bf16[288,896]{1,0:T(8,128)(2,1)S(1)} collective-permute-done((bf16[288,896]{1,0:T(8,128)(2,1)S(1)}, bf16[288,896]{1,0:T(8,128)(2,1)S(1)}, u32[]{:S(2)}, u32[]{:S(2)}) %collective-permute-start.40) | collective-permute-done | bytes 516128 | tf_op jit(solution)/shard_map/ppermute | solution.py:21
  214.9 2.5 fusion.72
  217.5 2.3 add_add_fusion
  219.8 9.3 %collective-permute-done.42 = bf16[288,896]{1,0:T(8,128)(2,1)} collective-permute-done((bf16[288,896]{1,0:T(8,128)(2,1)}, bf16[288,896]{1,0:T(8,128)(2,1)}, u32[]{:S(2)}, u32[]{:S(2)}) %collective-permute-start.42) | collective-permute-done | bytes 516128 | tf_op jit(solution)/shard_map/ppermute | solution.py:21
  230.9 2.4 fusion.68
  233.3 2.5 add_convert_fusion
  235.9 5.8 %collective-permute-start.44 = (bf16[36,1024]{1,0:T(8,128)(2,1)S(1)}, bf16[36,1024]{1,0:T(8,128)(2,1)S(1)}, u32[]{:S(2)}, u32[]{:S(2)}) collective-permute-start(bf16[36,1024]{1,0:T(8,128)(2,1)S(1)} %get-tuple-element.46), channel_id=1, source_target_pairs={{0,28},{4,0},{8,4},{12,8},{16,12},{20,16},{24,20},{28,24},{1,29},{... | collective-permute-start | bytes 221192 | tf_op jit(solution)/shard_map/ppermute | solution.py:26
  241.9 2.7 %collective-permute-start.47 = (bf16[36,1024]{1,0:T(8,128)(2,1)S(1)}, bf16[36,1024]{1,0:T(8,128)(2,1)S(1)}, u32[]{:S(2)}, u32[]{:S(2)}) collective-permute-start(bf16[36,1024]{1,0:T(8,128)(2,1)S(1)} %get-tuple-element.43), channel_id=1, source_target_pairs={{0,16},{4,20},{8,24},{12,28},{16,0},{20,4},{24,8},{28,12},{1,17},{... | collective-permute-start | bytes 221192 | tf_op jit(solution)/shard_map/ppermute | solution.py:26
  244.9 2.9 %collective-permute-start.49 = (bf16[36,1024]{1,0:T(8,128)(2,1)S(1)}, bf16[36,1024]{1,0:T(8,128)(2,1)S(1)}, u32[]{:S(2)}, u32[]{:S(2)}) collective-permute-start(bf16[36,1024]{1,0:T(8,128)(2,1)S(1)} %get-tuple-element.41), channel_id=1, source_target_pairs={{0,8},{4,12},{8,16},{12,20},{16,24},{20,28},{24,0},{28,4},{1,9},{5... | collective-permute-start | bytes 221192 | tf_op jit(solution)/shard_map/ppermute | solution.py:26
  248.2 8.8 %collective-permute-done.47 = bf16[36,1024]{1,0:T(8,128)(2,1)S(1)} collective-permute-done((bf16[36,1024]{1,0:T(8,128)(2,1)S(1)}, bf16[36,1024]{1,0:T(8,128)(2,1)S(1)}, u32[]{:S(2)}, u32[]{:S(2)}) %collective-permute-start.47) | collective-permute-done | bytes 73760 | tf_op jit(solution)/shard_map/ppermute | solution.py:26
  257.0 1.9 collective-permute-done.48
  260.8 2.4 multiply_reduce_fusion
  (185 shorter events, 47.2 us)
Async XLA Ops:
  2.1 10.6 %collective-permute-start = (bf16[3,1056]{0,1:T(8,128)(2,1)S(1)}, bf16[3,1056]{0,1:T(8,128)(2,1)S(1)}, u32[]{:S(2)}, u32[]{:S(2)}) collective-permute-start(bf16[3,1056]{0,1:T(8,128)(2,1)S(1)} %fusion.128), channel_id=1, source_target_pairs={{0,4},{4,8},{8,12},{12,16},{16,20},{20,24},{24,28},{1,5},{5,9},{9,... | collective-permute-start | bytes 19016 | tf_op jit(solution)/shard_map/ppermute | solution.py:17
  14.8 16.0 %collective-permute-start.1 = (bf16[17,1024]{1,0:T(8,128)(2,1)S(1)}, bf16[17,1024]{1,0:T(8,128)(2,1)S(1)}, u32[]{:S(2)}, u32[]{:S(2)}) collective-permute-start(bf16[17,1024]{1,0:T(8,128)(2,1)S(1)} %pad_maximum_fusion.3), channel_id=1, source_target_pairs={{0,4},{4,8},{8,12},{12,16},{16,20},{20,24},{24,28},{1,5},{5,9},{9,... | collective-permute-start | bytes 104456 | tf_op jit(solution)/shard_map/ppermute | solution.py:17
  19.3 13.1 %collective-permute-start.2 = (bf16[17,1024]{1,0:T(8,128)(2,1)S(1)}, bf16[17,1024]{1,0:T(8,128)(2,1)S(1)}, u32[]{:S(2)}, u32[]{:S(2)}) collective-permute-start(bf16[17,1024]{1,0:T(8,128)(2,1)S(1)} %pad_maximum_fusion.3), channel_id=1, source_target_pairs={{0,8},{4,12},{8,16},{12,20},{16,24},{20,28},{1,9},{5,13},{9,17},{1... | collective-permute-start | bytes 104456 | tf_op jit(solution)/shard_map/ppermute | solution.py:17
  22.8 10.9 %collective-permute-start.3 = (bf16[17,1024]{1,0:T(8,128)(2,1)S(1)}, bf16[17,1024]{1,0:T(8,128)(2,1)S(1)}, u32[]{:S(2)}, u32[]{:S(2)}) collective-permute-start(bf16[17,1024]{1,0:T(8,128)(2,1)S(1)} %pad_maximum_fusion.3), channel_id=1, source_target_pairs={{0,12},{4,16},{8,20},{12,24},{16,28},{1,13},{5,17},{9,21},{13,25},... | collective-permute-start | bytes 104456 | tf_op jit(solution)/shard_map/ppermute | solution.py:17
  28.2 5.6 %collective-permute-start.4 = (bf16[17,1024]{1,0:T(8,128)(2,1)S(1)}, bf16[17,1024]{1,0:T(8,128)(2,1)S(1)}, u32[]{:S(2)}, u32[]{:S(2)}) collective-permute-start(bf16[17,1024]{1,0:T(8,128)(2,1)S(1)} %pad_maximum_fusion.3), channel_id=1, source_target_pairs={{0,16},{4,20},{8,24},{12,28},{1,17},{5,21},{9,25},{13,29},{2,18},{... | collective-permute-start | bytes 104456 | tf_op jit(solution)/shard_map/ppermute | solution.py:17
  29.5 4.3 %collective-permute-start.5 = (bf16[17,1024]{1,0:T(8,128)(2,1)S(1)}, bf16[17,1024]{1,0:T(8,128)(2,1)S(1)}, u32[]{:S(2)}, u32[]{:S(2)}) collective-permute-start(bf16[17,1024]{1,0:T(8,128)(2,1)S(1)} %pad_maximum_fusion.3), channel_id=1, source_target_pairs={{0,20},{4,24},{8,28},{1,21},{5,25},{9,29},{2,22},{6,26},{10,30},{3... | collective-permute-start | bytes 104456 | tf_op jit(solution)/shard_map/ppermute | solution.py:17
  30.8 3.0 %collective-permute-start.6 = (bf16[17,1024]{1,0:T(8,128)(2,1)S(1)}, bf16[17,1024]{1,0:T(8,128)(2,1)S(1)}, u32[]{:S(2)}, u32[]{:S(2)}) collective-permute-start(bf16[17,1024]{1,0:T(8,128)(2,1)S(1)} %pad_maximum_fusion.3), channel_id=1, source_target_pairs={{0,24},{4,28},{1,25},{5,29},{2,26},{6,30},{3,27},{7,31}} | collective-permute-start | bytes 104456 | tf_op jit(solution)/shard_map/ppermute | solution.py:17
  32.4 3.0 %collective-permute-start.7 = (bf16[17,1024]{1,0:T(8,128)(2,1)S(1)}, bf16[17,1024]{1,0:T(8,128)(2,1)S(1)}, u32[]{:S(2)}, u32[]{:S(2)}) collective-permute-start(bf16[17,1024]{1,0:T(8,128)(2,1)S(1)} %pad_maximum_fusion.3), channel_id=1, source_target_pairs={{0,28},{1,29},{2,30},{3,31}} | collective-permute-start | bytes 104456 | tf_op jit(solution)/shard_map/ppermute | solution.py:17
  39.3 11.1 %collective-permute-start.9 = (bf16[128,1024]{1,0:T(8,128)(2,1)S(1)}, bf16[128,1024]{1,0:T(8,128)(2,1)S(1)}, u32[]{:S(2)}, u32[]{:S(2)}) collective-permute-start(bf16[128,1024]{1,0:T(8,128)(2,1)S(1)} %get-tuple-element.39), channel_id=1, source_target_pairs={{0,8},{4,12},{8,16},{12,20},{16,24},{20,28},{24,0},{28,4},{1,9},{5... | collective-permute-start | bytes 786440 | tf_op jit(solution)/shard_map/ppermute | solution.py:26
  39.4 19.0 %collective-permute-start.11 = (bf16[128,1024]{1,0:T(8,128)(2,1)S(1)}, bf16[128,1024]{1,0:T(8,128)(2,1)S(1)}, u32[]{:S(2)}, u32[]{:S(2)}) collective-permute-start(bf16[128,1024]{1,0:T(8,128)(2,1)S(1)} %get-tuple-element.39), channel_id=1, source_target_pairs={{0,16},{4,20},{8,24},{12,28},{16,0},{20,4},{24,8},{28,12},{1,17},{... | collective-permute-start | bytes 786440 | tf_op jit(solution)/shard_map/ppermute | solution.py:26
  42.5 17.7 %collective-permute-start.13 = (bf16[128,1024]{1,0:T(8,128)(2,1)S(1)}, bf16[128,1024]{1,0:T(8,128)(2,1)S(1)}, u32[]{:S(2)}, u32[]{:S(2)}) collective-permute-start(bf16[128,1024]{1,0:T(8,128)(2,1)S(1)} %get-tuple-element.39), channel_id=1, source_target_pairs={{0,24},{4,28},{8,0},{12,4},{16,8},{20,12},{24,16},{28,20},{1,25},{... | collective-permute-start | bytes 786440 | tf_op jit(solution)/shard_map/ppermute | solution.py:26
  43.2 17.2 %collective-permute-start.8 = (bf16[128,1024]{1,0:T(8,128)(2,1)S(1)}, bf16[128,1024]{1,0:T(8,128)(2,1)S(1)}, u32[]{:S(2)}, u32[]{:S(2)}) collective-permute-start(bf16[128,1024]{1,0:T(8,128)(2,1)S(1)} %get-tuple-element.39), channel_id=1, source_target_pairs={{0,4},{4,0},{8,12},{12,8},{16,20},{20,16},{24,28},{28,24},{1,5},{5... | collective-permute-start | bytes 786440 | tf_op jit(solution)/shard_map/ppermute | solution.py:133
  50.4 10.4 %collective-permute-start.10 = (bf16[128,1024]{1,0:T(8,128)(2,1)S(1)}, bf16[128,1024]{1,0:T(8,128)(2,1)S(1)}, u32[]{:S(2)}, u32[]{:S(2)}) collective-permute-start(bf16[128,1024]{1,0:T(8,128)(2,1)S(1)} %collective-permute-done.9), channel_id=1, source_target_pairs={{0,4},{4,0},{8,12},{12,8},{16,20},{20,16},{24,28},{28,24},{1,5},{5... | collective-permute-start | bytes 786440 | tf_op jit(solution)/shard_map/ppermute | solution.py:133
  58.3 9.2 %collective-permute-start.12 = (bf16[128,1024]{1,0:T(8,128)(2,1)S(1)}, bf16[128,1024]{1,0:T(8,128)(2,1)S(1)}, u32[]{:S(2)}, u32[]{:S(2)}) collective-permute-start(bf16[128,1024]{1,0:T(8,128)(2,1)S(1)} %collective-permute-done.11), channel_id=1, source_target_pairs={{0,4},{4,0},{8,12},{12,8},{16,20},{20,16},{24,28},{28,24},{1,5},{5... | collective-permute-start | bytes 786440 | tf_op jit(solution)/shard_map/ppermute | solution.py:133
  60.2 12.0 %collective-permute-start.14 = (bf16[128,1024]{1,0:T(8,128)(2,1)S(1)}, bf16[128,1024]{1,0:T(8,128)(2,1)S(1)}, u32[]{:S(2)}, u32[]{:S(2)}) collective-permute-start(bf16[128,1024]{1,0:T(8,128)(2,1)S(1)} %collective-permute-done.13), channel_id=1, source_target_pairs={{0,4},{4,0},{8,12},{12,8},{16,20},{20,16},{24,28},{28,24},{1,5},{5... | collective-permute-start | bytes 786440 | tf_op jit(solution)/shard_map/ppermute | solution.py:133
  73.8 5.7 %collective-permute-start.15 = (bf16[256,512]{1,0:T(8,128)(2,1)S(1)}, bf16[256,512]{1,0:T(8,128)(2,1)S(1)}, u32[]{:S(2)}, u32[]{:S(2)}) collective-permute-start(bf16[256,512]{1,0:T(8,128)(2,1)S(1)} %get-tuple-element.34), channel_id=1, source_target_pairs={{0,1},{1,0},{2,3},{3,2},{4,5},{5,4},{6,7},{7,6},{8,9},{9,8},{10,11... | collective-permute-start | bytes 786440 | tf_op jit(solution)/shard_map/ppermute | solution.py:21
  75.7 8.4 %collective-permute-start.17 = (bf16[256,512]{1,0:T(8,128)(2,1)S(1)}, bf16[256,512]{1,0:T(8,128)(2,1)S(1)}, u32[]{:S(2)}, u32[]{:S(2)}) collective-permute-start(bf16[256,512]{1,0:T(8,128)(2,1)S(1)} %fusion.117), channel_id=1, source_target_pairs={{0,2},{1,3},{2,0},{3,1},{4,6},{5,7},{6,4},{7,5},{8,10},{9,11},{10,... | collective-permute-start | bytes 786440 | tf_op jit(solution)/shard_map/ppermute | solution.py:21
  77.6 9.1 %collective-permute-start.20 = (f32[128]{0:T(128)S(1)}, f32[128]{0:T(128)S(1)}, u32[]{:S(2)}, u32[]{:S(2)}) collective-permute-start(f32[128]{0:T(128)S(1)} %get-tuple-element.38), channel_id=1, source_target_pairs={{0,1},{1,0},{2,3},{3,2},{4,5},{5,4},{6,7},{7,6},{8,9},{9,8},{10,11... | collective-permute-start | bytes 1544 | tf_op jit(solution)/shard_map/ppermute | solution.py:21
  77.7 9.0 %collective-permute-start.21 = (f32[128]{0:T(128)S(1)}, f32[128]{0:T(128)S(1)}, u32[]{:S(2)}, u32[]{:S(2)}) collective-permute-start(f32[128]{0:T(128)S(1)} %get-tuple-element.38), channel_id=1, source_target_pairs={{0,2},{1,3},{2,0},{3,1},{4,6},{5,7},{6,4},{7,5},{8,10},{9,11},{10,... | collective-permute-start | bytes 1544 | tf_op jit(solution)/shard_map/ppermute | solution.py:21
  78.3 8.5 %collective-permute-start.22 = (f32[128]{0:T(128)S(1)}, f32[128]{0:T(128)S(1)}, u32[]{:S(2)}, u32[]{:S(2)}) collective-permute-start(f32[128]{0:T(128)S(1)} %get-tuple-element.38), channel_id=1, source_target_pairs={{0,3},{1,2},{2,1},{3,0},{4,7},{5,6},{6,5},{7,4},{8,11},{9,10},{10,... | collective-permute-start | bytes 1544 | tf_op jit(solution)/shard_map/ppermute | solution.py:21
  84.9 5.0 %collective-permute-start.19 = (bf16[128,512]{1,0:T(8,128)(2,1)S(1)}, bf16[128,512]{1,0:T(8,128)(2,1)S(1)}, u32[]{:S(2)}, u32[]{:S(2)}) collective-permute-start(bf16[128,512]{1,0:T(8,128)(2,1)S(1)} %get-tuple-element.60), channel_id=1, source_target_pairs={{0,4},{1,12},{2,20},{3,28},{4,0},{5,8},{6,16},{7,24},{8,5},{9,13},... | collective-permute-start | bytes 393224 | tf_op jit(solution)/shard_map/ppermute | solution.py:171
  90.3 15.4 %collective-permute-start.23 = (f32[128]{0:T(128)S(1)}, f32[128]{0:T(128)S(1)}, u32[]{:S(2)}, u32[]{:S(2)}) collective-permute-start(f32[128]{0:T(128)S(1)} %fusion.101), channel_id=1, source_target_pairs={{0,1},{1,0},{2,3},{3,2},{4,5},{5,4},{6,7},{7,6},{8,9},{9,8},{10,11... | collective-permute-start | bytes 1544 | tf_op jit(solution)/shard_map/ppermute | solution.py:21
  96.2 10.9 %collective-permute-start.24 = (f32[128]{0:T(128)S(1)}, f32[128]{0:T(128)S(1)}, u32[]{:S(2)}, u32[]{:S(2)}) collective-permute-start(f32[128]{0:T(128)S(1)} %fusion.101), channel_id=1, source_target_pairs={{0,2},{1,3},{2,0},{3,1},{4,6},{5,7},{6,4},{7,5},{8,10},{9,11},{10,... | collective-permute-start | bytes 1544 | tf_op jit(solution)/shard_map/ppermute | solution.py:21
  105.6 3.0 %collective-permute-start.25 = (f32[128]{0:T(128)S(1)}, f32[128]{0:T(128)S(1)}, u32[]{:S(2)}, u32[]{:S(2)}) collective-permute-start(f32[128]{0:T(128)S(1)} %fusion.101), channel_id=1, source_target_pairs={{0,3},{1,2},{2,1},{3,0},{4,7},{5,6},{6,5},{7,4},{8,11},{9,10},{10,... | collective-permute-start | bytes 1544 | tf_op jit(solution)/shard_map/ppermute | solution.py:21
  109.1 8.2 %collective-permute-start.26 = (bf16[36,1024]{1,0:T(8,128)(2,1)S(1)}, bf16[36,1024]{1,0:T(8,128)(2,1)S(1)}, u32[]{:S(2)}, u32[]{:S(2)}) collective-permute-start(bf16[36,1024]{1,0:T(8,128)(2,1)S(1)} %get-tuple-element.53), channel_id=1, source_target_pairs={{0,4},{4,8},{8,12},{12,16},{16,20},{20,24},{24,28},{28,0},{1,5},{5... | collective-permute-start | bytes 221192 | tf_op jit(solution)/shard_map/ppermute | solution.py:26
  109.4 8.0 %collective-permute-start.27 = (bf16[36,1024]{1,0:T(8,128)(2,1)S(1)}, bf16[36,1024]{1,0:T(8,128)(2,1)S(1)}, u32[]{:S(2)}, u32[]{:S(2)}) collective-permute-start(bf16[36,1024]{1,0:T(8,128)(2,1)S(1)} %get-tuple-element.52), channel_id=1, source_target_pairs={{0,8},{4,12},{8,16},{12,20},{16,24},{20,28},{24,0},{28,4},{1,9},{5... | collective-permute-start | bytes 221192 | tf_op jit(solution)/shard_map/ppermute | solution.py:26
  110.1 13.5 %collective-permute-start.28 = (bf16[36,1024]{1,0:T(8,128)(2,1)S(1)}, bf16[36,1024]{1,0:T(8,128)(2,1)S(1)}, u32[]{:S(2)}, u32[]{:S(2)}) collective-permute-start(bf16[36,1024]{1,0:T(8,128)(2,1)S(1)} %get-tuple-element.51), channel_id=1, source_target_pairs={{0,12},{4,16},{8,20},{12,24},{16,28},{20,0},{24,4},{28,8},{1,13},{... | collective-permute-start | bytes 221192 | tf_op jit(solution)/shard_map/ppermute | solution.py:26
  110.7 12.8 %collective-permute-start.29 = (bf16[36,1024]{1,0:T(8,128)(2,1)S(1)}, bf16[36,1024]{1,0:T(8,128)(2,1)S(1)}, u32[]{:S(2)}, u32[]{:S(2)}) collective-permute-start(bf16[36,1024]{1,0:T(8,128)(2,1)S(1)} %get-tuple-element.50), channel_id=1, source_target_pairs={{0,16},{4,20},{8,24},{12,28},{16,0},{20,4},{24,8},{28,12},{1,17},{... | collective-permute-start | bytes 221192 | tf_op jit(solution)/shard_map/ppermute | solution.py:26
  115.1 8.5 %collective-permute-start.30 = (bf16[36,1024]{1,0:T(8,128)(2,1)S(1)}, bf16[36,1024]{1,0:T(8,128)(2,1)S(1)}, u32[]{:S(2)}, u32[]{:S(2)}) collective-permute-start(bf16[36,1024]{1,0:T(8,128)(2,1)S(1)} %get-tuple-element.49), channel_id=1, source_target_pairs={{0,20},{4,24},{8,28},{12,0},{16,4},{20,8},{24,12},{28,16},{1,21},{... | collective-permute-start | bytes 221192 | tf_op jit(solution)/shard_map/ppermute | solution.py:26
  117.2 7.8 %collective-permute-start.31 = (bf16[36,1024]{1,0:T(8,128)(2,1)S(1)}, bf16[36,1024]{1,0:T(8,128)(2,1)S(1)}, u32[]{:S(2)}, u32[]{:S(2)}) collective-permute-start(bf16[36,1024]{1,0:T(8,128)(2,1)S(1)} %get-tuple-element.48), channel_id=1, source_target_pairs={{0,24},{4,28},{8,0},{12,4},{16,8},{20,12},{24,16},{28,20},{1,25},{... | collective-permute-start | bytes 221192 | tf_op jit(solution)/shard_map/ppermute | solution.py:26
  117.4 7.6 %collective-permute-start.32 = (bf16[36,1024]{1,0:T(8,128)(2,1)S(1)}, bf16[36,1024]{1,0:T(8,128)(2,1)S(1)}, u32[]{:S(2)}, u32[]{:S(2)}) collective-permute-start(bf16[36,1024]{1,0:T(8,128)(2,1)S(1)} %get-tuple-element.47), channel_id=1, source_target_pairs={{0,28},{4,0},{8,4},{12,8},{16,12},{20,16},{24,20},{28,24},{1,29},{... | collective-permute-start | bytes 221192 | tf_op jit(solution)/shard_map/ppermute | solution.py:26
  129.4 2.7 %collective-permute-start.33 = (bf16[288,1792]{1,0:T(8,128)(2,1)S(1)}, bf16[288,1792]{1,0:T(8,128)(2,1)S(1)}, u32[]{:S(2)}, u32[]{:S(2)}) collective-permute-start(bf16[288,1792]{1,0:T(8,128)(2,1)S(1)} %fusion.42), channel_id=1, source_target_pairs={{0,1},{1,0},{2,3},{3,2},{4,5},{5,4},{6,7},{7,6},{8,9},{9,8},{10,11... | collective-permute-start | bytes 3096584 | tf_op jit(solution)/shard_map/ppermute | solution.py:21
  140.6 9.3 %collective-permute-start.34 = (bf16[288,1792]{1,0:T(8,128)(2,1)}, bf16[288,1792]{1,0:T(8,128)(2,1)}, u32[]{:S(2)}, u32[]{:S(2)}) collective-permute-start(bf16[288,1792]{1,0:T(8,128)(2,1)} %fusion.45), channel_id=1, source_target_pairs={{0,1},{1,0},{2,3},{3,2},{4,5},{5,4},{6,7},{7,6},{8,9},{9,8},{10,11... | collective-permute-start | bytes 3096584 | tf_op jit(solution)/shard_map/ppermute | solution.py:21
  145.0 18.3 %collective-permute-start.35 = (bf16[288,1792]{1,0:T(8,128)(2,1)}, bf16[288,1792]{1,0:T(8,128)(2,1)S(1)}, u32[]{:S(2)}, u32[]{:S(2)}) collective-permute-start(bf16[288,1792]{1,0:T(8,128)(2,1)} %fusion.54), channel_id=1, source_target_pairs={{0,1},{1,0},{2,3},{3,2},{4,5},{5,4},{6,7},{7,6},{8,9},{9,8},{10,11... | collective-permute-start | bytes 3096584 | tf_op jit(solution)/shard_map/ppermute | solution.py:21
  149.6 13.7 %collective-permute-start.37 = (bf16[288,1792]{1,0:T(8,128)(2,1)}, bf16[288,1792]{1,0:T(8,128)(2,1)S(1)}, u32[]{:S(2)}, u32[]{:S(2)}) collective-permute-start(bf16[288,1792]{1,0:T(8,128)(2,1)} %fusion.63), channel_id=1, source_target_pairs={{0,1},{1,0},{2,3},{3,2},{4,5},{5,4},{6,7},{7,6},{8,9},{9,8},{10,11... | collective-permute-start | bytes 3096584 | tf_op jit(solution)/shard_map/ppermute | solution.py:21
  149.7 25.9 %collective-permute-start.36 = (bf16[288,1792]{1,0:T(8,128)(2,1)}, bf16[288,1792]{1,0:T(8,128)(2,1)S(1)}, u32[]{:S(2)}, u32[]{:S(2)}) collective-permute-start(bf16[288,1792]{1,0:T(8,128)(2,1)} %fusion.39), channel_id=1, source_target_pairs={{0,2},{1,3},{2,0},{3,1},{4,6},{5,7},{6,4},{7,5},{8,10},{9,11},{10,... | collective-permute-start | bytes 3096584 | tf_op jit(solution)/shard_map/ppermute | solution.py:21
  154.6 42.7 %collective-permute-start.38 = (bf16[288,1792]{1,0:T(8,128)(2,1)}, bf16[288,1792]{1,0:T(8,128)(2,1)}, u32[]{:S(2)}, u32[]{:S(2)}) collective-permute-start(bf16[288,1792]{1,0:T(8,128)(2,1)} %fusion.36), channel_id=1, source_target_pairs={{0,2},{1,3},{2,0},{3,1},{4,6},{5,7},{6,4},{7,5},{8,10},{9,11},{10,... | collective-permute-start | bytes 3096584 | tf_op jit(solution)/shard_map/ppermute | solution.py:21
  200.5 14.1 %collective-permute-start.40 = (bf16[288,896]{1,0:T(8,128)(2,1)S(1)}, bf16[288,896]{1,0:T(8,128)(2,1)S(1)}, u32[]{:S(2)}, u32[]{:S(2)}) collective-permute-start(bf16[288,896]{1,0:T(8,128)(2,1)S(1)} %get-tuple-element.37), channel_id=1, source_target_pairs={{0,2},{1,3},{2,0},{3,1},{4,6},{5,7},{6,4},{7,5},{8,10},{9,11},{10,... | collective-permute-start | bytes 1548296 | tf_op jit(solution)/shard_map/ppermute | solution.py:21
  214.7 2.8 %collective-permute-start.41 = (bf16[288,896]{1,0:T(8,128)(2,1)S(1)}, bf16[288,896]{1,0:T(8,128)(2,1)S(1)}, u32[]{:S(2)}, u32[]{:S(2)}) collective-permute-start(bf16[288,896]{1,0:T(8,128)(2,1)S(1)} %collective-permute-done.40), channel_id=1, source_target_pairs={{0,1},{1,0},{2,3},{3,2},{4,5},{5,4},{6,7},{7,6},{8,9},{9,8},{10,11... | collective-permute-start | bytes 1548296 | tf_op jit(solution)/shard_map/ppermute | solution.py:21
  214.7 14.5 %collective-permute-start.42 = (bf16[288,896]{1,0:T(8,128)(2,1)}, bf16[288,896]{1,0:T(8,128)(2,1)}, u32[]{:S(2)}, u32[]{:S(2)}) collective-permute-start(bf16[288,896]{1,0:T(8,128)(2,1)} %get-tuple-element.36), channel_id=1, source_target_pairs={{0,2},{1,3},{2,0},{3,1},{4,6},{5,7},{6,4},{7,5},{8,10},{9,11},{10,... | collective-permute-start | bytes 1548296 | tf_op jit(solution)/shard_map/ppermute | solution.py:21
  229.1 4.2 %collective-permute-start.43 = (bf16[288,896]{1,0:T(8,128)(2,1)}, bf16[288,896]{1,0:T(8,128)(2,1)}, u32[]{:S(2)}, u32[]{:S(2)}) collective-permute-start(bf16[288,896]{1,0:T(8,128)(2,1)} %collective-permute-done.42), channel_id=1, source_target_pairs={{0,1},{1,0},{2,3},{3,2},{4,5},{5,4},{6,7},{7,6},{8,9},{9,8},{10,11... | collective-permute-start | bytes 1548296 | tf_op jit(solution)/shard_map/ppermute | solution.py:21
  235.9 9.0 %collective-permute-start.44 = (bf16[36,1024]{1,0:T(8,128)(2,1)S(1)}, bf16[36,1024]{1,0:T(8,128)(2,1)S(1)}, u32[]{:S(2)}, u32[]{:S(2)}) collective-permute-start(bf16[36,1024]{1,0:T(8,128)(2,1)S(1)} %get-tuple-element.46), channel_id=1, source_target_pairs={{0,28},{4,0},{8,4},{12,8},{16,12},{20,16},{24,20},{28,24},{1,29},{... | collective-permute-start | bytes 221192 | tf_op jit(solution)/shard_map/ppermute | solution.py:26
  241.7 6.1 %collective-permute-start.45 = (bf16[36,1024]{1,0:T(8,128)(2,1)S(1)}, bf16[36,1024]{1,0:T(8,128)(2,1)S(1)}, u32[]{:S(2)}, u32[]{:S(2)}) collective-permute-start(bf16[36,1024]{1,0:T(8,128)(2,1)S(1)} %get-tuple-element.45), channel_id=1, source_target_pairs={{0,24},{4,28},{8,0},{12,4},{16,8},{20,12},{24,16},{28,20},{1,25},{... | collective-permute-start | bytes 221192 | tf_op jit(solution)/shard_map/ppermute | solution.py:26
  241.7 6.5 %collective-permute-start.46 = (bf16[36,1024]{1,0:T(8,128)(2,1)S(1)}, bf16[36,1024]{1,0:T(8,128)(2,1)S(1)}, u32[]{:S(2)}, u32[]{:S(2)}) collective-permute-start(bf16[36,1024]{1,0:T(8,128)(2,1)S(1)} %get-tuple-element.44), channel_id=1, source_target_pairs={{0,20},{4,24},{8,28},{12,0},{16,4},{20,8},{24,12},{28,16},{1,21},{... | collective-permute-start | bytes 221192 | tf_op jit(solution)/shard_map/ppermute | solution.py:26
  241.9 15.0 %collective-permute-start.47 = (bf16[36,1024]{1,0:T(8,128)(2,1)S(1)}, bf16[36,1024]{1,0:T(8,128)(2,1)S(1)}, u32[]{:S(2)}, u32[]{:S(2)}) collective-permute-start(bf16[36,1024]{1,0:T(8,128)(2,1)S(1)} %get-tuple-element.43), channel_id=1, source_target_pairs={{0,16},{4,20},{8,24},{12,28},{16,0},{20,4},{24,8},{28,12},{1,17},{... | collective-permute-start | bytes 221192 | tf_op jit(solution)/shard_map/ppermute | solution.py:26
  244.7 14.2 %collective-permute-start.48 = (bf16[36,1024]{1,0:T(8,128)(2,1)S(1)}, bf16[36,1024]{1,0:T(8,128)(2,1)S(1)}, u32[]{:S(2)}, u32[]{:S(2)}) collective-permute-start(bf16[36,1024]{1,0:T(8,128)(2,1)S(1)} %get-tuple-element.42), channel_id=1, source_target_pairs={{0,12},{4,16},{8,20},{12,24},{16,28},{20,0},{24,4},{28,8},{1,13},{... | collective-permute-start | bytes 221192 | tf_op jit(solution)/shard_map/ppermute | solution.py:26
  244.9 14.0 %collective-permute-start.49 = (bf16[36,1024]{1,0:T(8,128)(2,1)S(1)}, bf16[36,1024]{1,0:T(8,128)(2,1)S(1)}, u32[]{:S(2)}, u32[]{:S(2)}) collective-permute-start(bf16[36,1024]{1,0:T(8,128)(2,1)S(1)} %get-tuple-element.41), channel_id=1, source_target_pairs={{0,8},{4,12},{8,16},{12,20},{16,24},{20,28},{24,0},{28,4},{1,9},{5... | collective-permute-start | bytes 221192 | tf_op jit(solution)/shard_map/ppermute | solution.py:26
  247.7 11.1 %collective-permute-start.50 = (bf16[36,1024]{1,0:T(8,128)(2,1)S(1)}, bf16[36,1024]{1,0:T(8,128)(2,1)S(1)}, u32[]{:S(2)}, u32[]{:S(2)}) collective-permute-start(bf16[36,1024]{1,0:T(8,128)(2,1)S(1)} %get-tuple-element.40), channel_id=1, source_target_pairs={{0,4},{4,8},{8,12},{12,16},{16,20},{20,24},{24,28},{28,0},{1,5},{5... | collective-permute-start | bytes 221192 | tf_op jit(solution)/shard_map/ppermute | solution.py:26
  (17 other events, 220.6 us)
